TPU v7x, 128 devices: a whole 4x4x4 slice. The times are simulated.
128 devices in a mesh: file: 4 (over z), rows: 32 (over x, y, core).
Axes of the slice: x: 4, y: 4, z: 4, core: 2. Of those that a mesh axis runs over, the one named last changes fastest.
Arguments:
- snapshots: float32 [16384, 2048], P('rows', 'file'), may hold values from -4000 to 4000
- part_map: int32 [16384], replicated, may hold values from 0 to 16383, as said below
- jac_blocks: float32 [16384, 8, 4096], P(('file', 'rows')), may hold values from -2 to 8
- jac_cols: int32 [16384, 8], P(('file', 'rows')), may hold values from -1 to 16383, as said below
Outputs:
- basis: float32 [16384, 2048], P(('file', 'rows'))
- jac_basis: float32 [16384, 2048], P(('file', 'rows'))
- reduced: float32 [32, 32], replicated
Inputs may be any that keep to these rules, and one draw needn't show every extreme that they name: `part_map`: A permutation of the cell blocks. The 128 slots of each partition hold exactly 1 block of each group of 128 consecutive cell blocks, in no particular order. `jac_cols`: in each row, entry 0 is the row's own slot s, the valid entries come first and -1 pads the rest; each row has 3 to 8 valid entries and some row has 8. Every valid entry lies in the partition of s, in the last 32 slots of the partition before it, or in the first 32 slots of the partition after it.
All inputs are finite; a program needn't handle non-finite values.
Results may differ from a plain program's by a relative error of at most 0.0001.
Values sent between devices are 32-bit elements; how exact they have to be, the bound alone decides.
No kernel may reach another device: no remote copies, remote signals or barrier semaphores. Data moves between devices by JAX's collectives and lax.ppermute only.
A program may use at most 192 MiB of HBM per device.

v0:
```python
import jax
import jax.numpy as jnp
from jax import lax
from jax.experimental import pallas as pl
from jax.experimental.pallas import tpu as pltpu
from jax.sharding import PartitionSpec as P

NSNAP = 32
BS = 64
NNZB = 8
RIM = 32
HALF = NSNAP // 2
LANES = 128
AXES = ("file", "rows")
VMEM = pltpu.VMEM
SMEM = pltpu.SMEM
NT = (((1,), (1,)), ((), ()))
HIGH = lax.Precision.HIGHEST


def spec(space):
    return pl.BlockSpec(memory_space=space)


def limit(mib):
    return pltpu.CompilerParams(vmem_limit_bytes=mib * 1024 * 1024)


def cost(flops, nbytes):
    return pl.CostEstimate(flops=flops, bytes_accessed=nbytes, transcendentals=0)


def low_half(shape):
    return lax.broadcasted_iota(jnp.int32, shape, len(shape) - 1) < BS


def split_pair(first, second):
    low = low_half(first.shape)
    zero = jnp.where(low, first, pltpu.roll(second, BS, 1))
    one = jnp.where(low, pltpu.roll(first, BS, 1), second)
    return zero, one


def pack_kernel(rows_ref, snap_ref, out_ref):
    per_pair = out_ref.shape[1] // 4

    def body(part, carry):
        for q in range(per_pair):
            row = rows_ref[part * per_pair + q]
            out_ref[part, 4 * q : 4 * q + 4, :] = snap_ref[pl.ds(row, 4, stride=8), :]
        return carry

    lax.fori_loop(0, out_ref.shape[0], body, 0, unroll=4)


def pack(snapshots, rows, n_part):
    blocks, width = snapshots.shape
    tiles = width // LANES
    view = snapshots.reshape(blocks // 8, 8, tiles, LANES).transpose(0, 2, 1, 3)
    view = view.reshape(blocks * tiles, LANES)
    per_pair = blocks // n_part
    return pl.pallas_call(
        pack_kernel,
        out_shape=jax.ShapeDtypeStruct((n_part, per_pair * tiles, LANES), jnp.float32),
        in_specs=[spec(SMEM), spec(VMEM)],
        out_specs=spec(VMEM),
        name="pack",
    )(rows, view)


def split_kernel(jac_ref, high_ref, low_ref):
    def body(s, carry):
        for pair in range(NNZB // 2):
            for tb in range(2):
                first = jac_ref[s, pl.ds(tb * 128 + 2 * pair, 16, stride=8), :]
                second = jac_ref[s, pl.ds(tb * 128 + 2 * pair + 1, 16, stride=8), :]
                for r2, part in enumerate(split_pair(first, second)):
                    high = part.astype(jnp.bfloat16)
                    low = (part - high.astype(jnp.float32)).astype(jnp.bfloat16)
                    where = (s, slice(32 * r2 + 16 * tb, 32 * r2 + 16 * tb + 16), slice(128 * pair, 128 * pair + 128))
                    high_ref[where] = high
                    low_ref[where] = low
        return carry

    lax.fori_loop(0, jac_ref.shape[0], body, 0)


def split_blocks(jac_blocks):
    slots = jac_blocks.shape[0]
    view = jac_blocks.reshape(slots, NNZB, BS * BS // LANES, LANES).transpose(0, 2, 1, 3)
    view = view.reshape(slots, NNZB * BS * BS // LANES, LANES)
    step = 8
    out = jax.ShapeDtypeStruct((slots, BS, NNZB * BS), jnp.bfloat16)
    return pl.pallas_call(
        split_kernel,
        out_shape=(out, out),
        grid=(slots // step,),
        in_specs=[pl.BlockSpec((step,) + view.shape[1:], lambda i: (i, 0, 0))],
        out_specs=[pl.BlockSpec((step,) + out.shape[1:], lambda i: (i, 0, 0))] * 2,
        cost_estimate=cost(0, 32 * 1024 * 1024),
        name="split_blocks",
    )(view)


def assemble_kernel(rows_ref, recv_ref, snap_ref, pairs_ref, gram_ref):
    slots = snap_ref.shape[0]
    per_file = recv_ref.shape[0] // 4

    def body(s, carry):
        row = rows_ref[s]
        for f in range(4):
            snap_ref[s, 4 * f : 4 * f + 4, :] = recv_ref[pl.ds(f * per_file + row, 4), :]
        return carry

    lax.fori_loop(0, slots, body, 0, unroll=4)
    for sp in range(slots // 2):
        zero, one = split_pair(snap_ref[2 * sp], snap_ref[2 * sp + 1])
        pairs_ref[0:HALF, sp * LANES : sp * LANES + LANES] = zero
        pairs_ref[HALF:NSNAP, sp * LANES : sp * LANES + LANES] = one
    pairs = pairs_ref[...]
    gram_ref[...] = lax.dot_general(pairs, pairs, NT, precision=HIGH, preferred_element_type=jnp.float32)


def assemble(received, rows, slots):
    return pl.pallas_call(
        assemble_kernel,
        out_shape=(
            jax.ShapeDtypeStruct((slots, HALF, LANES), jnp.float32),
            jax.ShapeDtypeStruct((NSNAP, slots * BS), jnp.float32),
            jax.ShapeDtypeStruct((NSNAP, NSNAP), jnp.float32),
        ),
        in_specs=[spec(SMEM), spec(VMEM)],
        out_specs=(spec(VMEM),) * 3,
        name="assemble",
    )(rows, received.reshape(-1, LANES))


def apply_kernel(cols_ref, lo_ref, own_ref, hi_ref, pairs_ref, jh_ref, jl_ref, out_ref, red_ref, xh_ref, xl_ref):
    g = pl.program_id(0)
    low16 = low_half((HALF, LANES))

    @pl.when(g == 0)
    def _():
        def fill(ref, base, count):
            def body(s, carry):
                x = ref[s]
                y = pltpu.roll(x, BS, 1)
                for kk, part in enumerate((jnp.where(low16, x, y), jnp.where(low16, y, x))):
                    high = part.astype(jnp.bfloat16)
                    low = (part - high.astype(jnp.float32)).astype(jnp.bfloat16)
                    xh_ref[base + s, HALF * kk : HALF * kk + HALF, :] = high
                    xl_ref[base + s, HALF * kk : HALF * kk + HALF, :] = low
                return carry

            lax.fori_loop(0, count, body, 0, unroll=2)

        slots = own_ref.shape[0]
        fill(lo_ref, 0, RIM)
        fill(own_ref, RIM, slots)
        fill(hi_ref, RIM + slots, RIM)
        xh_ref[slots + 2 * RIM] = jnp.zeros((NSNAP, LANES), jnp.bfloat16)
        xl_ref[slots + 2 * RIM] = jnp.zeros((NSNAP, LANES), jnp.bfloat16)
        red_ref[...] = jnp.zeros_like(red_ref)

    low32 = low_half((NSNAP, LANES))
    lane = lax.broadcasted_iota(jnp.int32, (NSNAP, LANES), 1)
    r = lane % BS
    order = lane - r + (r % 2) * (BS // 2) + r // 2
    group = 4
    for sub in range(jh_ref.shape[0] // group):
        highs, lows = [], []
        for i in range(group):
            hi_parts, lo_parts = [], []
            for pair in range(NNZB // 2):
                at = ((g * (jh_ref.shape[0]) + sub * group + i) * NNZB) + 2 * pair
                a = cols_ref[at]
                b = cols_ref[at + 1]
                hi_parts.append(jnp.where(low32, xh_ref[a], xh_ref[b]))
                lo_parts.append(jnp.where(low32, xl_ref[a], xl_ref[b]))
            highs.append(jnp.concatenate(hi_parts, axis=1))
            lows.append(jnp.concatenate(lo_parts, axis=1))
        high = jnp.concatenate(highs, axis=0)
        both = jnp.concatenate(highs + lows, axis=0)
        jh = jh_ref[sub * group : sub * group + group].reshape(group * BS, NNZB * BS)
        jl = jl_ref[sub * group : sub * group + group].reshape(group * BS, NNZB * BS)
        big = lax.dot_general(both, jh, NT, preferred_element_type=jnp.float32)
        acc = big[0 : group * NSNAP] + big[group * NSNAP :]
        acc = acc + lax.dot_general(high, jl, NT, preferred_element_type=jnp.float32)
        outs = []
        for ip in range(group // 2):
            tile = acc[:, LANES * ip : LANES * ip + LANES]
            top = tile[2 * ip * NSNAP : 2 * ip * NSNAP + NSNAP]
            bottom = tile[2 * ip * NSNAP + NSNAP : 2 * ip * NSNAP + 2 * NSNAP]
            mixed = jnp.where(low32, top, bottom)
            mixed = jnp.take_along_axis(mixed, order, axis=1)
            outs.append(mixed)
            first, second = split_pair(mixed[0:HALF], mixed[HALF:NSNAP])
            out_ref[sub * group + 2 * ip] = first
            out_ref[sub * group + 2 * ip + 1] = second
        width = group // 2 * LANES
        red_ref[...] += lax.dot_general(
            pairs_ref[:, sub * width : sub * width + width],
            jnp.concatenate(outs, axis=1),
            NT,
            precision=HIGH,
            preferred_element_type=jnp.float32,
        )


def apply_blocks(cols, lo, own, hi, pairs, jac_high, jac_low):
    slots = own.shape[0]
    step = 8
    block = (step, BS, NNZB * BS)
    whole = lambda shape: pl.BlockSpec(shape, lambda i: (0,) * len(shape))
    return pl.pallas_call(
        apply_kernel,
        out_shape=(
            jax.ShapeDtypeStruct((slots, HALF, LANES), jnp.float32),
            jax.ShapeDtypeStruct((NSNAP, NSNAP), jnp.float32),
        ),
        grid=(slots // step,),
        in_specs=[
            spec(SMEM),
            whole(lo.shape),
            whole(own.shape),
            whole(hi.shape),
            pl.BlockSpec((NSNAP, step * BS), lambda i: (0, i)),
            pl.BlockSpec(block, lambda i: (i, 0, 0)),
            pl.BlockSpec(block, lambda i: (i, 0, 0)),
        ],
        out_specs=(
            pl.BlockSpec((step, HALF, LANES), lambda i: (i, 0, 0)),
            whole((NSNAP, NSNAP)),
        ),
        scratch_shapes=[
            pltpu.VMEM((slots + 2 * RIM + 1, NSNAP, LANES), jnp.bfloat16),
            pltpu.VMEM((slots + 2 * RIM + 1, NSNAP, LANES), jnp.bfloat16),
        ],
        compiler_params=limit(32),
        cost_estimate=cost(2 * 3 * slots * 4 * NSNAP * 512 * BS, 24 * 1024 * 1024),
        name="apply_blocks",
    )(cols, lo, own, hi, pairs, jac_high, jac_low)


def factor_kernel(total_rows, gram_ref, scaled_ref):
    row = lax.broadcasted_iota(jnp.int32, (NSNAP, LANES), 0)
    lane = lax.broadcasted_iota(jnp.int32, (NSNAP, LANES), 1)
    rank = 2 * (row % HALF) + row // HALF
    unit = jnp.where(lane - NSNAP == row, 1.0, 0.0).astype(jnp.float32)
    work = jnp.concatenate([gram_ref[...], jnp.zeros((NSNAP, LANES - NSNAP), jnp.float32)], axis=1) + unit
    for k in range(NSNAP):
        at = (k % 2) * HALF + k // 2
        pivot_row = jnp.broadcast_to(work[at : at + 1, :], (NSNAP, LANES))
        pivot_col = jnp.broadcast_to(work[:, at : at + 1], (NSNAP, LANES))
        pivot = jnp.broadcast_to(work[at : at + 1, at : at + 1], (NSNAP, LANES))
        ratio = jnp.where(rank > k, pivot_col / pivot, 0.0)
        work = work - ratio * pivot_row
    diag = jnp.sum(jnp.where(lane == row, work, 0.0), axis=1, keepdims=True)
    scale = float(total_rows) ** 0.5 / jnp.sqrt(diag)
    scaled_ref[...] = (pltpu.roll(work, LANES - NSNAP, 1) * scale)[:, 0:NSNAP]


def factor(gram, total_rows):
    return pl.pallas_call(
        lambda *refs: factor_kernel(total_rows, *refs),
        out_shape=jax.ShapeDtypeStruct((NSNAP, NSNAP), jnp.float32),
        in_specs=[spec(VMEM)],
        out_specs=spec(VMEM),
        cost_estimate=cost(32 * 32 * 128 * 4, 8192),
        name="factor",
    )(gram)


def mix_kernel(scaled_ref, snap_ref, jac_ref, basis_ref, out_ref, same_ref, swap_ref):
    low = low_half((HALF, LANES))

    @pl.when(pl.program_id(0) == 0)
    def _():
        scaled = scaled_ref[...]
        wide = lambda rows, j: jnp.broadcast_to(scaled[rows * HALF : rows * HALF + HALF, j : j + 1], (HALF, LANES))
        for j2 in range(HALF):
            same_ref[j2] = jnp.where(low, wide(0, j2), wide(1, HALF + j2))
            swap_ref[j2] = jnp.where(low, wide(0, HALF + j2), wide(1, j2))

    for source, target in ((snap_ref, basis_ref), (jac_ref, out_ref)):
        for s8 in range(target.shape[0] // 8):
            plain = [source[pl.ds(s8 * 8 * HALF + j2, 8, stride=HALF), :] for j2 in range(HALF)]
            turned = [pltpu.roll(x, BS, 1) for x in plain]
            for k2 in range(HALF):
                total = None
                for j2 in range(k2 + 1):
                    for coef, value in ((same_ref, plain[j2]), (swap_ref, turned[j2])):
                        term = jnp.broadcast_to(coef[j2, k2 : k2 + 1, :], (8, LANES)) * value
                        total = term if total is None else total + term
                target[8 * s8 : 8 * s8 + 8, LANES * k2 : LANES * k2 + LANES] = total


def mix(scaled, snaps, jac):
    slots = snaps.shape[0]
    step = 16
    out = jax.ShapeDtypeStruct((slots, NSNAP * BS), jnp.float32)
    flat = lambda x: x.reshape(slots * HALF, LANES)
    return pl.pallas_call(
        mix_kernel,
        out_shape=(out, out),
        grid=(slots // step,),
        in_specs=[
            pl.BlockSpec((NSNAP, NSNAP), lambda i: (0, 0)),
            pl.BlockSpec((step * HALF, LANES), lambda i: (i, 0)),
            pl.BlockSpec((step * HALF, LANES), lambda i: (i, 0)),
        ],
        out_specs=[pl.BlockSpec((step, NSNAP * BS), lambda i: (i, 0))] * 2,
        scratch_shapes=[pltpu.VMEM((HALF, HALF, LANES), jnp.float32)] * 2,
        cost_estimate=cost(2 * 2 * slots * BS * NSNAP * NSNAP, 4 * 1024 * 1024),
        name="mix",
    )(scaled, flat(snaps), flat(jac))


def finish_kernel(total_rows, scaled_ref, red_ref, out_ref):
    row = lax.broadcasted_iota(jnp.int32, (NSNAP, NSNAP), 0)
    col = lax.broadcasted_iota(jnp.int32, (NSNAP, NSNAP), 1)
    place = jnp.where(col == (row % 2) * HALF + row // 2, 1.0, 0.0).astype(jnp.float32)
    dot = lambda a, b, dims: lax.dot_general(a, b, dims, precision=HIGH, preferred_element_type=jnp.float32)
    nn = (((1,), (0,)), ((), ()))
    natural = dot(place, scaled_ref[...], nn)
    out_ref[...] = dot(dot(natural, red_ref[...], nn), natural, NT) / float(total_rows)


def finish(scaled, reduced, total_rows):
    return pl.pallas_call(
        lambda *refs: finish_kernel(total_rows, *refs),
        out_shape=jax.ShapeDtypeStruct((NSNAP, NSNAP), jnp.float32),
        in_specs=[spec(VMEM)] * 2,
        out_specs=spec(VMEM),
        name="finish",
    )(scaled, reduced)


def total_over_devices(block, n_part):
    copies = jnp.broadcast_to(block.reshape(1, 8, LANES), (n_part, 8, LANES))
    copies = lax.all_to_all(copies, AXES, split_axis=0, concat_axis=0, tiled=True)
    return jnp.sum(copies, axis=0).reshape(NSNAP, NSNAP)


def shards(snapshots, part_map, jac_blocks, jac_cols):
    n_file = lax.axis_size("file")
    n_rows = lax.axis_size("rows")
    n_part = n_file * n_rows
    file_pos = lax.axis_index("file")
    rows_pos = lax.axis_index("rows")
    blocks = jac_blocks.shape[0]
    held = snapshots.shape[0]
    per_pair = held // blocks
    total_rows = blocks * BS * n_part
    my_part = file_pos * n_rows + rows_pos

    local = part_map.reshape(n_part, blocks) - rows_pos * held
    group = jnp.arange(per_pair, dtype=jnp.int32)
    taken = jnp.sum(jnp.where((local >> 7)[:, None, :] == group[None, :, None], local[:, None, :], 0), axis=2)
    send_rows = ((taken >> 3) * 32 + (taken & 7)).reshape(n_part * per_pair)
    packed = pack(snapshots, send_rows, n_part)
    received = lax.all_to_all(packed, AXES, split_axis=0, concat_axis=0, tiled=True)

    jac_high, jac_low = split_blocks(jac_blocks)
    received, jac_high, jac_low = lax.optimization_barrier((received, jac_high, jac_low))

    my_slots = lax.dynamic_slice_in_dim(part_map, my_part * blocks, blocks)
    recv_rows = (my_slots // held) * (4 * per_pair) + ((my_slots >> 7) % per_pair) * 4
    snaps, pairs, part_gram = assemble(received, recv_rows, blocks)

    forward = [(i, i + 1) for i in range(n_part - 1)]
    backward = [(b, a) for a, b in forward]
    lo = lax.ppermute(snaps[blocks - RIM :], AXES, forward)
    hi = lax.ppermute(snaps[:RIM], AXES, backward)
    gram = total_over_devices(part_gram, n_part)

    extended = blocks + 2 * RIM
    where = jnp.clip(jac_cols - (my_part * blocks - RIM), 0, extended - 1)
    cols = jnp.where(jac_cols >= 0, where, extended).reshape(blocks * NNZB)
    jac_snaps, part_reduced = apply_blocks(cols, lo, snaps, hi, pairs, jac_high, jac_low)

    reduced = total_over_devices(part_reduced, n_part)
    scaled = factor(gram, total_rows)
    basis, jac_basis = mix(scaled, snaps, jac_snaps)
    return basis, jac_basis, finish(scaled, reduced, total_rows)


def solution(mesh):
    in_specs = (P("rows", "file"), P(), P(AXES, None, None), P(AXES, None))
    out_specs = (P(AXES, None), P(AXES, None), P())
    return jax.shard_map(shards, mesh=mesh, in_specs=in_specs, out_specs=out_specs, check_vma=False)
```

profile of v0, /device:TPU:1, one launch (start us, length us, event | category | flops | bytes accessed | tf_op | source)
XLA Modules:
  0.0 130.7 jit_solution(5233383954450705616)
XLA Ops:
  0.6 0.9 broadcast_shift-right-arithmetic_fusion
  1.5 0.1 select_reduce_fusion
  1.6 0.1 copy.8
  1.8 0.7 add.29.rows_ref
  2.5 2.9 %pack.1 = f32[128,16,128]{2,1,0:T(8,128)} custom-call(s32[512]{0:T(512)} %add.29.rows_ref, f32[2048,128]{1,0:T(8,128)} %bitcast.20), custom_call_target="tpu_custom_call" | custom-call | tf_op jit(solution)/shard_map/pack/pallas_call | solution.py:62
  5.3 11.5 %all-to-all-start = ((f32[128,16,128]{2,1,0:T(8,128)}), f32[128,16,128]{2,1,0:T(8,128)S(1)}, u32[]{:S(2)}, u32[]{:S(2)}) async-start(f32[128,16,128]{2,1,0:T(8,128)} %pack.1), calls=%async_computation | async-start | bytes 2097152 | tf_op jit(solution)/shard_map/all_to_all | solution.py:362
  16.8 0.0 copy-start.6
  16.8 21.8 %split_blocks.1 = (bf16[128,64,512]{2,1,0:T(8,128)(2,1)}, bf16[128,64,512]{2,1,0:T(8,128)(2,1)}) custom-call(f32[128,256,128]{2,1,0:T(8,128)} %bitcast.18), custom_call_target="tpu_custom_call" | custom-call | bytes 33554432 | tf_op jit(solution)/shard_map/split_blocks/pallas_call | solution.py:94
  38.6 1.3 fusion.1.rows_ref
  39.9 0.0 all-to-all-done
  39.9 0.0 copy-start.5
  39.9 1.0 copy-done.5
  40.9 3.4 %assemble.1 = (f32[128,16,128]{2,1,0:T(8,128)}, f32[32,8192]{1,0:T(8,128)}, f32[32,32]{1,0:T(8,128)}) custom-call(s32[128]{0:T(128)} %fusion.1.rows_ref, f32[2048,128]{1,0:T(8,128)} %bitcast.19), custom_call_target="tpu_custom_call" | custom-call | tf_op jit(solution)/shard_map/assemble/pallas_call | solution.py:125
  44.3 1.1 fusion.3
  45.4 3.0 %collective-permute-start.1 = (f32[32,16,128]{2,1,0:T(8,128)S(1)}, f32[32,16,128]{2,1,0:T(8,128)S(1)}, u32[]{:S(2)}, u32[]{:S(2)}) collective-permute-start(f32[32,16,128]{2,1,0:T(8,128)S(1)} %get-tuple-element.29), channel_id=1, source_target_pairs={{1,0},{2,1},{3,2},{4,3},{5,4},{6,5},{7,6},{8,7},{9,8},{10,9},{11,1... | collective-permute-start | bytes 786440 | tf_op jit(solution)/shard_map/ppermute | solution.py:374
  48.4 2.6 %collective-permute-start = (f32[32,16,128]{2,1,0:T(8,128)S(1)}, f32[32,16,128]{2,1,0:T(8,128)S(1)}, u32[]{:S(2)}, u32[]{:S(2)}) collective-permute-start(f32[32,16,128]{2,1,0:T(8,128)S(1)} %get-tuple-element.30), channel_id=1, source_target_pairs={{0,1},{1,2},{2,3},{3,4},{4,5},{5,6},{6,7},{7,8},{8,9},{9,10},{10,1... | collective-permute-start | bytes 786440 | tf_op jit(solution)/shard_map/ppermute | solution.py:373
  51.0 0.8 broadcast_in_dim.35
  51.8 0.8 broadcast_in_dim.36
  52.6 13.2 %all-to-all-start.1 = ((f32[128,8,128]{2,1,0:T(8,128)}), f32[128,8,128]{2,1,0:T(8,128)S(1)}, u32[]{:S(2)}, u32[]{:S(2)}) async-start(f32[128,8,128]{2,1,0:T(8,128)} %broadcast_in_dim.36), calls=%async_computation.1 | async-start | bytes 1048576 | tf_op jit(solution)/shard_map/all_to_all | solution.py:341
  65.8 0.0 copy-done.6
  65.9 0.1 copy.9
  66.0 0.1 reshape.68.cols_ref
  66.1 0.0 collective-permute-done.1.hi_ref
  66.1 0.0 collective-permute-done.lo_ref
  66.1 0.0 copy-start
  66.1 3.4 %copy-done = bf16[128,64,512]{2,1,0:T(8,128)(2,1)S(1)} copy-done((bf16[128,64,512]{2,1,0:T(8,128)(2,1)S(1)}, bf16[128,64,512]{2,1,0:T(8,128)(2,1)}, u32[]{:S(2)}) %copy-start) | copy-done | bytes 8388632
  69.5 0.0 copy-start.1
  69.5 3.4 %copy-done.1 = bf16[128,64,512]{2,1,0:T(8,128)(2,1)S(1)} copy-done((bf16[128,64,512]{2,1,0:T(8,128)(2,1)S(1)}, bf16[128,64,512]{2,1,0:T(8,128)(2,1)}, u32[]{:S(2)}) %copy-start.1) | copy-done | bytes 8388632
  72.8 0.0 copy-start.2
  72.8 1.2 copy-done.2
  74.1 0.0 copy-start.4
  74.1 1.2 copy-done.4
  75.3 27.5 %apply_blocks.1 = (f32[128,16,128]{2,1,0:T(8,128)S(1)}, f32[32,32]{1,0:T(8,128)S(1)}) custom-call(s32[1024]{0:T(1024)S(1)} %reshape.68.cols_ref, f32[32,16,128]{2,1,0:T(8,128)S(1)} %collective-permute-done.lo_ref, f32[128,16,128]{2,1,0:T(8,128)S(1)} %copy-done.2, f32[32,16,128]{2,1,0:T(8,128)S(1)} %collective-permute-done.1.hi_ref, ...), custom_call_target="tpu_custom_call" | custom-call | flops 3221225472 | bytes 25165824 | tf_op jit(solution)/shard_map/apply_blocks/pallas_call | solution.py:215
  102.8 0.0 copy-start.3
  102.9 1.0 copy-done.3
  103.8 0.1 broadcast_in_dim.38
  103.9 0.0 all-to-all-done.1
  103.9 0.8 broadcast_in_dim.39
  104.7 9.8 %all-to-all-start.2 = ((f32[128,8,128]{2,1,0:T(8,128)}), f32[128,8,128]{2,1,0:T(8,128)S(1)}, u32[]{:S(2)}, u32[]{:S(2)}) async-start(f32[128,8,128]{2,1,0:T(8,128)} %broadcast_in_dim.39), calls=%async_computation.2 | async-start | bytes 1048576 | tf_op jit(solution)/shard_map/all_to_all | solution.py:341
  114.5 0.1 reduce_sum.28
  114.7 0.7 reshape.66.refs_0_
  115.3 5.3 %factor.1.scaled_ref.refs_0_ = f32[32,32]{1,0:T(8,128)} custom-call(f32[32,32]{1,0:T(8,128)} %reshape.66.refs_0_), custom_call_target="tpu_custom_call" | custom-call | flops 524288 | bytes 8192 | tf_op jit(solution)/shard_map/factor/pallas_call | solution.py:264
  120.6 7.5 %mix.1 = (f32[128,2048]{1,0:T(8,128)}, f32[128,2048]{1,0:T(8,128)}) custom-call(f32[32,32]{1,0:T(8,128)} %factor.1.scaled_ref.refs_0_, f32[2048,128]{1,0:T(8,128)} %bitcast.16, f32[2048,128]{1,0:T(8,128)} %bitcast.17), custom_call_target="tpu_custom_call" | custom-call | flops 33554432 | bytes 4194304 | tf_op jit(solution)/shard_map/mix/pallas_call | solution.py:303
  128.1 0.0 all-to-all-done.2
  128.1 0.1 reduce_sum.29
  128.3 0.7 reshape.70.refs_1_
  128.9 1.8 %finish.1 = f32[32,32]{1,0:T(8,128)} custom-call(f32[32,32]{1,0:T(8,128)} %factor.1.scaled_ref.refs_0_, f32[32,32]{1,0:T(8,128)} %reshape.70.refs_1_), custom_call_target="tpu_custom_call" | custom-call | tf_op jit(solution)/shard_map/finish/pallas_call | solution.py:330
  (2 shorter events, 0.0 us)
Async XLA Ops:
  5.3 34.6 %all-to-all-start = ((f32[128,16,128]{2,1,0:T(8,128)}), f32[128,16,128]{2,1,0:T(8,128)S(1)}, u32[]{:S(2)}, u32[]{:S(2)}) async-start(f32[128,16,128]{2,1,0:T(8,128)} %pack.1), calls=%async_computation | async-start | bytes 2097152 | tf_op jit(solution)/shard_map/all_to_all | solution.py:362
  16.8 49.0 %copy-start.6 = (s32[128,8]{0,1:T(8,128)S(1)}, s32[128,8]{0,1:T(8,128)}, u32[]{:S(2)}) copy-start(s32[128,8]{0,1:T(8,128)} %param.7) | copy-start | bytes 12292
  39.9 1.0 copy-start.5
  45.4 20.7 %collective-permute-start.1 = (f32[32,16,128]{2,1,0:T(8,128)S(1)}, f32[32,16,128]{2,1,0:T(8,128)S(1)}, u32[]{:S(2)}, u32[]{:S(2)}) collective-permute-start(f32[32,16,128]{2,1,0:T(8,128)S(1)} %get-tuple-element.29), channel_id=1, source_target_pairs={{1,0},{2,1},{3,2},{4,3},{5,4},{6,5},{7,6},{8,7},{9,8},{10,9},{11,1... | collective-permute-start | bytes 786440 | tf_op jit(solution)/shard_map/ppermute | solution.py:374
  48.4 17.7 %collective-permute-start = (f32[32,16,128]{2,1,0:T(8,128)S(1)}, f32[32,16,128]{2,1,0:T(8,128)S(1)}, u32[]{:S(2)}, u32[]{:S(2)}) collective-permute-start(f32[32,16,128]{2,1,0:T(8,128)S(1)} %get-tuple-element.30), channel_id=1, source_target_pairs={{0,1},{1,2},{2,3},{3,4},{4,5},{5,6},{6,7},{7,8},{8,9},{9,10},{10,1... | collective-permute-start | bytes 786440 | tf_op jit(solution)/shard_map/ppermute | solution.py:373
  52.6 51.3 %all-to-all-start.1 = ((f32[128,8,128]{2,1,0:T(8,128)}), f32[128,8,128]{2,1,0:T(8,128)S(1)}, u32[]{:S(2)}, u32[]{:S(2)}) async-start(f32[128,8,128]{2,1,0:T(8,128)} %broadcast_in_dim.36), calls=%async_computation.1 | async-start | bytes 1048576 | tf_op jit(solution)/shard_map/all_to_all | solution.py:341
  66.1 3.4 %copy-start = (bf16[128,64,512]{2,1,0:T(8,128)(2,1)S(1)}, bf16[128,64,512]{2,1,0:T(8,128)(2,1)}, u32[]{:S(2)}) copy-start(bf16[128,64,512]{2,1,0:T(8,128)(2,1)} %get-tuple-element.21.jh_ref) | copy-start | bytes 25165828
  69.5 3.4 %copy-start.1 = (bf16[128,64,512]{2,1,0:T(8,128)(2,1)S(1)}, bf16[128,64,512]{2,1,0:T(8,128)(2,1)}, u32[]{:S(2)}) copy-start(bf16[128,64,512]{2,1,0:T(8,128)(2,1)} %get-tuple-element.22.jl_ref) | copy-start | bytes 25165828
  72.8 1.2 copy-start.2
  74.1 1.2 copy-start.4
  102.8 1.0 copy-start.3
  104.7 23.4 %all-to-all-start.2 = ((f32[128,8,128]{2,1,0:T(8,128)}), f32[128,8,128]{2,1,0:T(8,128)S(1)}, u32[]{:S(2)}, u32[]{:S(2)}) async-start(f32[128,8,128]{2,1,0:T(8,128)} %broadcast_in_dim.39), calls=%async_computation.2 | async-start | bytes 1048576 | tf_op jit(solution)/shard_map/all_to_all | solution.py:341
where the time goes:
time: 132 us; the launch traced here: 131 us
  Pallas kernels  70.2 us (53%)
  starting transfers between devices  40.1 us (30%)
  local copies, waits for them, and re-layouts  17.1 us (13%)
  other arithmetic  2.57 us (2%)
    pallas_call x1, Pallas kernels, apply_blocks(): pl.pallas_call(apply_kernel, out_shape=(jax.ShapeDtypeStruct((slots, HALF...  27.5 us
    all_to_all x2, starting transfers between devices, total_over_devices(): lax.all_to_all(copies, AXES, split_axis=0, concat_axis=0, tiled=True)  23 us
    pallas_call x1, Pallas kernels, split_blocks(): pl.pallas_call(split_kernel, out_shape=(out, out), grid=(slots // step,),...  21.8 us
    all_to_all x1, starting transfers between devices, shards(): lax.all_to_all(packed, AXES, split_axis=0, concat_axis=0, tiled=True)  11.5 us
    unnamed x14, local copies, waits for them, and re-layouts  11.1 us
    pallas_call x1, Pallas kernels, mix(): pl.pallas_call(mix_kernel, out_shape=(out, out), grid=(slots // step,), i...  7.5 us
    pallas_call x1, Pallas kernels, factor(): pl.pallas_call(lambda *refs: factor_kernel(total_rows, *refs), out_shape=...  5.29 us
    pallas_call x1, Pallas kernels, assemble(): pl.pallas_call(assemble_kernel, out_shape=(jax.ShapeDtypeStruct((slots, H...  3.45 us
  transfers between devices with their start and end apart: 5, of which 0 were waited for; matrix products, arithmetic and copies ran while one was open for 3% of the time, Pallas kernels for 48%

commit v1 on v0

v1 whole, which is shorter than its diff:
```python
import jax
import jax.numpy as jnp
from jax import lax
from jax.experimental import pallas as pl
from jax.experimental.pallas import tpu as pltpu
from jax.sharding import PartitionSpec as P

NSNAP = 32
BS = 64
NNZB = 8
RIM = 32
HALF = NSNAP // 2
LANES = 128
AXES = ("file", "rows")
VMEM = pltpu.VMEM
SMEM = pltpu.SMEM
NT = (((1,), (1,)), ((), ()))
HIGH = lax.Precision.HIGHEST


def spec(space):
    return pl.BlockSpec(memory_space=space)


def limit(mib):
    return pltpu.CompilerParams(vmem_limit_bytes=mib * 1024 * 1024)


def cost(flops, nbytes):
    return pl.CostEstimate(flops=flops, bytes_accessed=nbytes, transcendentals=0)


def low_half(shape):
    return lax.broadcasted_iota(jnp.int32, shape, len(shape) - 1) < BS


def split_pair(first, second):
    low = low_half(first.shape)
    zero = jnp.where(low, first, pltpu.roll(second, BS, 1))
    one = jnp.where(low, pltpu.roll(first, BS, 1), second)
    return zero, one


def send_copies(block, out_ref):
    tile = jnp.concatenate([block[8 * i : 8 * i + 8, 0:NSNAP] for i in range(4)], axis=1)
    for p in range(out_ref.shape[0]):
        out_ref[p] = tile


def sum_copies(ref):
    parts = [ref[p] for p in range(ref.shape[0])]
    while len(parts) > 1:
        parts = [x + y for x, y in zip(parts[0::2], parts[1::2])]
    tile = parts[0]
    return jnp.concatenate([tile] + [pltpu.roll(tile, LANES - NSNAP * i, 1) for i in range(1, 4)], axis=0)


def my_part():
    return lax.axis_index("file") * lax.axis_size("rows") + lax.axis_index("rows")


def pack_kernel(map_ref, snap_hbm, out_ref, recv_ref, snap_ref, index_ref, rows_ref, snap_sem, rows_sem):
    fetch = pltpu.make_async_copy(snap_hbm, snap_ref, snap_sem)
    fetch.start()
    n_part, slots = map_ref.shape
    per_pair = out_ref.shape[1] // 4
    held = slots * per_pair

    local = map_ref[...] - lax.axis_index("rows") * held
    group = local >> 7
    within = (local & 127).astype(jnp.float32)
    ones = jnp.ones((8, slots), jnp.bfloat16)
    for q in range(per_pair):
        part = jnp.where(group == q, within, 0.0).astype(jnp.bfloat16)
        found = lax.dot_general(ones, part, NT, preferred_element_type=jnp.float32)
        row = found[0:1].astype(jnp.int32) + q * slots
        index_ref[q : q + 1, :] = (row >> 3) * 32 + (row & 7)
    move = pltpu.make_async_copy(index_ref, rows_ref, rows_sem)
    move.start()

    mine = map_ref[pl.ds(my_part(), 1), :]
    recv_ref[...] = (mine >> 9) * (4 * per_pair) + ((mine >> 7) & (per_pair - 1)) * 4
    move.wait()
    fetch.wait()

    def body(part, carry):
        for q in range(per_pair):
            row = rows_ref[q, part]
            out_ref[part, 4 * q : 4 * q + 4, :] = snap_ref[pl.ds(row, 4, stride=8), :]
        return carry

    lax.fori_loop(0, n_part, body, 0, unroll=8)


def pack(snapshots, part_map, n_part):
    blocks, width = snapshots.shape
    tiles = width // LANES
    slots = part_map.shape[0] // n_part
    per_pair = blocks // slots
    assert slots == 128 and tiles == 4 and per_pair == 4
    view = snapshots.reshape(blocks // 8, 8, tiles, LANES).transpose(0, 2, 1, 3)
    view = view.reshape(blocks * tiles, LANES)
    return pl.pallas_call(
        pack_kernel,
        out_shape=(
            jax.ShapeDtypeStruct((n_part, per_pair * tiles, LANES), jnp.float32),
            jax.ShapeDtypeStruct((1, slots), jnp.int32),
        ),
        in_specs=[spec(VMEM), spec(pl.ANY)],
        out_specs=(spec(VMEM), spec(VMEM)),
        scratch_shapes=[
            pltpu.VMEM(view.shape, jnp.float32),
            pltpu.VMEM((per_pair, n_part), jnp.int32),
            pltpu.SMEM((per_pair, n_part), jnp.int32),
            pltpu.SemaphoreType.DMA,
            pltpu.SemaphoreType.DMA,
        ],
        compiler_params=limit(60),
        name="pack",
    )(part_map.reshape(n_part, slots), view)


def split_kernel(jac_ref, high_ref, low_ref):
    def body(s, carry):
        for pair in range(NNZB // 2):
            for tb in range(2):
                first = jac_ref[s, pl.ds(tb * 128 + 2 * pair, 16, stride=8), :]
                second = jac_ref[s, pl.ds(tb * 128 + 2 * pair + 1, 16, stride=8), :]
                for r2, part in enumerate(split_pair(first, second)):
                    high = part.astype(jnp.bfloat16)
                    low = (part - high.astype(jnp.float32)).astype(jnp.bfloat16)
                    rows = slice(32 * r2 + 16 * tb, 32 * r2 + 16 * tb + 16)
                    lanes = slice(LANES * pair, LANES * pair + LANES)
                    high_ref[s, rows, lanes] = high
                    low_ref[s, rows, lanes] = low
        return carry

    lax.fori_loop(0, jac_ref.shape[0], body, 0)


def split_blocks(jac_blocks):
    slots = jac_blocks.shape[0]
    view = jac_blocks.reshape(slots, NNZB, BS * BS // LANES, LANES).transpose(0, 2, 1, 3)
    view = view.reshape(slots, NNZB * BS * BS // LANES, LANES)
    step = 16
    out = jax.ShapeDtypeStruct((slots, BS, NNZB * BS), jnp.bfloat16)
    return pl.pallas_call(
        split_kernel,
        out_shape=(out, out),
        grid=(slots // step,),
        in_specs=[pl.BlockSpec((step,) + view.shape[1:], lambda i: (i, 0, 0))],
        out_specs=[pl.BlockSpec((step,) + out.shape[1:], lambda i: (i, 0, 0))] * 2,
        compiler_params=limit(48),
        cost_estimate=cost(0, 32 * 1024 * 1024),
        name="split_blocks",
    )(view)


def assemble_kernel(rows_ref, recv_ref, snap_ref, near_ref, far_ref):
    slots = snap_ref.shape[0]
    per_file = recv_ref.shape[0] // 4

    def body(s, carry):
        row = rows_ref[0, s]
        for f in range(4):
            snap_ref[s, 4 * f : 4 * f + 4, :] = recv_ref[pl.ds(f * per_file + row, 4), :]
        return carry

    lax.fori_loop(0, slots, body, 0, unroll=8)
    odd = my_part() % 2
    near_ref[...] = snap_ref[pl.ds((1 - odd) * (slots - RIM), RIM)]
    far_ref[...] = snap_ref[pl.ds(odd * (slots - RIM), RIM)]


def assemble(received, rows, slots):
    rim = jax.ShapeDtypeStruct((RIM, HALF, LANES), jnp.float32)
    return pl.pallas_call(
        assemble_kernel,
        out_shape=(jax.ShapeDtypeStruct((slots, HALF, LANES), jnp.float32), rim, rim),
        in_specs=[spec(SMEM), spec(VMEM)],
        out_specs=(spec(VMEM),) * 3,
        compiler_params=limit(6),
        name="assemble",
    )(rows, received.reshape(-1, LANES))


def make_pairs(snap_ref, pairs_ref):
    for sp in range(snap_ref.shape[0] // 2):
        zero, one = split_pair(snap_ref[2 * sp], snap_ref[2 * sp + 1])
        pairs_ref[0:HALF, sp * LANES : sp * LANES + LANES] = zero
        pairs_ref[HALF:NSNAP, sp * LANES : sp * LANES + LANES] = one


def gram_kernel(snap_ref, copies_ref, pairs_ref):
    make_pairs(snap_ref, pairs_ref)
    pairs = pairs_ref[...]
    gram = lax.dot_general(pairs, pairs, NT, precision=HIGH, preferred_element_type=jnp.float32)
    send_copies(gram, copies_ref)


def gram_part(snaps, n_part):
    slots = snaps.shape[0]
    return pl.pallas_call(
        gram_kernel,
        out_shape=jax.ShapeDtypeStruct((n_part, 8, LANES), jnp.float32),
        in_specs=[spec(VMEM)],
        out_specs=spec(VMEM),
        scratch_shapes=[pltpu.VMEM((NSNAP, slots * BS), jnp.float32)],
        compiler_params=limit(8),
        cost_estimate=cost(2 * 6 * NSNAP * NSNAP * slots * BS, 3 * 1024 * 1024),
        name="gram_part",
    )(snaps)


CHUNK = 16


def apply_kernel(cols_ref, near_ref, own_ref, far_ref, jh_hbm, jl_hbm, out_ref, copies_ref, xh_ref, xl_ref, pairs_ref, mixed_ref, jh_ref, jl_ref, sems):
    low16 = low_half((HALF, LANES))
    low32 = low_half((NSNAP, LANES))
    slots = own_ref.shape[0]

    def fetch(c):
        rows = pl.ds(c * CHUNK, CHUNK)
        return (
            pltpu.make_async_copy(jh_hbm.at[rows], jh_ref.at[rows], sems.at[0, c]),
            pltpu.make_async_copy(jl_hbm.at[rows], jl_ref.at[rows], sems.at[1, c]),
        )

    for c in range(slots // CHUNK):
        for copy in fetch(c):
            copy.start()

    def fill(ref, base, count):
        def body(s, carry):
            x = ref[s]
            y = pltpu.roll(x, BS, 1)
            for kk, part in enumerate((jnp.where(low16, x, y), jnp.where(low16, y, x))):
                high = part.astype(jnp.bfloat16)
                low = (part - high.astype(jnp.float32)).astype(jnp.bfloat16)
                xh_ref[base + s, HALF * kk : HALF * kk + HALF, :] = high
                xl_ref[base + s, HALF * kk : HALF * kk + HALF, :] = low
            return carry

        lax.fori_loop(0, count, body, 0, unroll=8)

    odd = my_part() % 2
    first_slot = my_part() * slots - RIM
    last_row = slots + 2 * RIM - 1
    fill(near_ref, (1 - odd) * (slots + RIM), RIM)
    fill(own_ref, RIM, slots)
    fill(far_ref, odd * (slots + RIM), RIM)
    xh_ref[last_row + 1] = jnp.zeros((NSNAP, LANES), jnp.bfloat16)
    xl_ref[last_row + 1] = jnp.zeros((NSNAP, LANES), jnp.bfloat16)
    make_pairs(own_ref, pairs_ref)

    def table_row(n, s):
        column = cols_ref[n, s]
        row = jnp.minimum(jnp.maximum(column - first_slot, 0), last_row)
        return jnp.where(column < 0, last_row + 1, row)

    lane = lax.broadcasted_iota(jnp.int32, (NSNAP, LANES), 1)
    r = lane % BS
    order = lane - r + (r % 2) * (BS // 2) + r // 2
    group = 4

    def body(g, carry):
        highs, lows = [], []
        for i in range(group):
            hi_parts, lo_parts = [], []
            for pair in range(NNZB // 2):
                a = table_row(2 * pair, g * group + i)
                b = table_row(2 * pair + 1, g * group + i)
                hi_parts.append(jnp.where(low32, xh_ref[a], xh_ref[b]))
                lo_parts.append(jnp.where(low32, xl_ref[a], xl_ref[b]))
            highs.append(jnp.concatenate(hi_parts, axis=1))
            lows.append(jnp.concatenate(lo_parts, axis=1))
        high = jnp.concatenate(highs, axis=0)
        both = jnp.concatenate(highs + lows, axis=0)
        jh = jh_ref[pl.ds(g * group, group)].reshape(group * BS, NNZB * BS)
        jl = jl_ref[pl.ds(g * group, group)].reshape(group * BS, NNZB * BS)
        big = lax.dot_general(both, jh, NT, preferred_element_type=jnp.float32)
        acc = big[0 : group * NSNAP] + big[group * NSNAP :]
        acc = acc + lax.dot_general(high, jl, NT, preferred_element_type=jnp.float32)
        for ip in range(group // 2):
            tile = acc[:, LANES * ip : LANES * ip + LANES]
            top = tile[2 * ip * NSNAP : 2 * ip * NSNAP + NSNAP]
            bottom = tile[2 * ip * NSNAP + NSNAP : 2 * ip * NSNAP + 2 * NSNAP]
            mixed = jnp.take_along_axis(jnp.where(low32, top, bottom), order, axis=1)
            mixed_ref[:, pl.ds(pl.multiple_of((g * 2 + ip) * LANES, LANES), LANES)] = mixed
            first, second = split_pair(mixed[0:HALF], mixed[HALF:NSNAP])
            out_ref[g * group + 2 * ip] = first
            out_ref[g * group + 2 * ip + 1] = second
        return carry

    def chunk(c, carry):
        for copy in fetch(c):
            copy.wait()
        per_chunk = CHUNK // group
        return lax.fori_loop(c * per_chunk, c * per_chunk + per_chunk, body, carry, unroll=True)

    lax.fori_loop(0, slots // CHUNK, chunk, 0)
    reduced = lax.dot_general(pairs_ref[...], mixed_ref[...], NT, precision=HIGH, preferred_element_type=jnp.float32)
    send_copies(reduced, copies_ref)


def apply_blocks(cols, near, own, far, jac_high, jac_low, n_part):
    slots = own.shape[0]
    table = pltpu.VMEM((slots + 2 * RIM + 1, NSNAP, LANES), jnp.bfloat16)
    wide = pltpu.VMEM((NSNAP, slots * BS), jnp.float32)
    held = pltpu.VMEM(jac_high.shape, jac_high.dtype)
    return pl.pallas_call(
        apply_kernel,
        out_shape=(
            jax.ShapeDtypeStruct((slots, HALF, LANES), jnp.float32),
            jax.ShapeDtypeStruct((n_part, 8, LANES), jnp.float32),
        ),
        in_specs=[spec(SMEM)] + [spec(VMEM)] * 3 + [spec(pl.ANY)] * 2,
        out_specs=(spec(VMEM),) * 2,
        scratch_shapes=[table, table, wide, wide, held, held, pltpu.SemaphoreType.DMA((2, slots // CHUNK))],
        compiler_params=limit(48),
        cost_estimate=cost(2 * 3 * slots * 4 * NSNAP * 512 * BS, 24 * 1024 * 1024),
        name="apply_blocks",
    )(cols, near, own, far, jac_high, jac_low)


def factor(gram, total_rows):
    row = lax.broadcasted_iota(jnp.int32, (NSNAP, LANES), 0)
    lane = lax.broadcasted_iota(jnp.int32, (NSNAP, LANES), 1)
    rank = 2 * (row % HALF) + row // HALF
    unit = jnp.where(lane - NSNAP == row, 1.0, 0.0).astype(jnp.float32)
    work = jnp.where(lane < NSNAP, gram, unit)
    wide = lambda x: jnp.broadcast_to(x, (NSNAP, LANES))
    for k2 in range(HALF):
        p, q = k2, HALF + k2
        row_p, row_q = wide(work[p : p + 1, :]), wide(work[q : q + 1, :])
        col_p, col_q = wide(work[:, p : p + 1]), wide(work[:, q : q + 1])
        a = wide(work[p : p + 1, p : p + 1])
        b = wide(work[q : q + 1, p : p + 1])
        c = wide(work[q : q + 1, q : q + 1])
        ratio = b / a
        row_q = row_q - ratio * row_p
        below = (col_p / a) * row_p + ((col_q - ratio * col_p) / (c - ratio * b)) * row_q
        work = work - jnp.where(rank > 2 * k2 + 1, below, jnp.where(rank == 2 * k2 + 1, ratio * row_p, 0.0))
    diag = jnp.sum(jnp.where(lane == row, work, 0.0), axis=1, keepdims=True)
    scale = float(total_rows) ** 0.5 / jnp.sqrt(diag)
    return pltpu.roll(work, LANES - NSNAP, 1) * scale


def mix_kernel(total_rows, gram_ref, snap_ref, jac_ref, basis_ref, out_ref, scaled_ref, same_ref, swap_ref, plain_ref, turned_ref):
    low = low_half((HALF, LANES))

    @pl.when(pl.program_id(0) == 0)
    def _():
        scaled = factor(sum_copies(gram_ref), total_rows)
        scaled_ref[...] = scaled[:, 0:NSNAP]
        wide = lambda kk, j: jnp.broadcast_to(scaled[kk * HALF : kk * HALF + HALF, j : j + 1], (HALF, LANES))
        for j2 in range(HALF):
            same_ref[j2] = jnp.where(low, wide(0, j2), wide(1, HALF + j2))
            swap_ref[j2] = jnp.where(low, wide(0, HALF + j2), wide(1, j2))

    both = range(2)
    for source, target in ((snap_ref, basis_ref), (jac_ref, out_ref)):
        def body(pair, carry):
            for j2 in range(HALF):
                for h in both:
                    x = source[pl.ds((2 * pair + h) * 8 * HALF + j2, 8, stride=HALF), :]
                    plain_ref[h, j2] = x
                    turned_ref[h, j2] = pltpu.roll(x, BS, 1)
            for k4 in range(0, HALF, 4):
                totals = {}
                for j2 in range(k4 + 4):
                    values = [(plain_ref[h, j2], turned_ref[h, j2]) for h in both]
                    for k2 in range(max(k4, j2), k4 + 4):
                        same = jnp.broadcast_to(same_ref[j2, k2 : k2 + 1, :], (8, LANES))
                        swap = jnp.broadcast_to(swap_ref[j2, k2 : k2 + 1, :], (8, LANES))
                        for h in both:
                            term = same * values[h][0] + swap * values[h][1]
                            totals[k2, h] = totals[k2, h] + term if j2 else term
                for k2 in range(k4, k4 + 4):
                    for h in both:
                        rows = pl.ds(pl.multiple_of((2 * pair + h) * 8, 8), 8)
                        target[rows, LANES * k2 : LANES * k2 + LANES] = totals[k2, h]
            return carry

        lax.fori_loop(0, target.shape[0] // 16, body, 0)


def mix(gram, snaps, jac, total_rows):
    slots = snaps.shape[0]
    step = 32
    out = jax.ShapeDtypeStruct((slots, NSNAP * BS), jnp.float32)
    flat = lambda x: x.reshape(slots * HALF, LANES)
    rows = pl.BlockSpec((step * HALF, LANES), lambda i: (i, 0))
    return pl.pallas_call(
        lambda *refs: mix_kernel(total_rows, *refs),
        out_shape=(out, out, jax.ShapeDtypeStruct((NSNAP, NSNAP), jnp.float32)),
        grid=(slots // step,),
        in_specs=[pl.BlockSpec(gram.shape, lambda i: (0, 0, 0)), rows, rows],
        out_specs=[pl.BlockSpec((step, NSNAP * BS), lambda i: (i, 0))] * 2 + [pl.BlockSpec((NSNAP, NSNAP), lambda i: (0, 0))],
        scratch_shapes=[pltpu.VMEM((HALF, HALF, LANES), jnp.float32)] * 2 + [pltpu.VMEM((2, HALF, 8, LANES), jnp.float32)] * 2,
        cost_estimate=cost(2 * 2 * slots * BS * NSNAP * NSNAP, 4 * 1024 * 1024),
        compiler_params=limit(12),
        name="mix",
    )(gram, flat(snaps), flat(jac))


def finish_kernel(total_rows, scaled_ref, red_ref, out_ref):
    row = lax.broadcasted_iota(jnp.int32, (NSNAP, NSNAP), 0)
    col = lax.broadcasted_iota(jnp.int32, (NSNAP, NSNAP), 1)
    place = jnp.where(col == (row % 2) * HALF + row // 2, 1.0, 0.0).astype(jnp.float32)
    dot = lambda a, b, dims: lax.dot_general(a, b, dims, precision=HIGH, preferred_element_type=jnp.float32)
    nn = (((1,), (0,)), ((), ()))
    natural = dot(place, scaled_ref[...], nn)
    reduced = sum_copies(red_ref)[:, 0:NSNAP]
    out_ref[...] = dot(dot(natural, reduced, nn), natural, NT) / float(total_rows)


def finish(scaled, reduced, total_rows):
    return pl.pallas_call(
        lambda *refs: finish_kernel(total_rows, *refs),
        out_shape=jax.ShapeDtypeStruct((NSNAP, NSNAP), jnp.float32),
        in_specs=[spec(VMEM)] * 2,
        out_specs=spec(VMEM),
        compiler_params=limit(4),
        name="finish",
    )(scaled, reduced)


def exchange(tiles):
    return lax.all_to_all(tiles, AXES, split_axis=0, concat_axis=0, tiled=True)


def shards(snapshots, part_map, jac_blocks, jac_cols):
    n_part = lax.axis_size("file") * lax.axis_size("rows")
    blocks = jac_blocks.shape[0]
    total_rows = blocks * BS * n_part

    packed, recv_rows = pack(snapshots, part_map, n_part)
    received = exchange(packed)
    jac_high, jac_low = split_blocks(jac_blocks)
    received, jac_high, jac_low = lax.optimization_barrier((received, jac_high, jac_low))
    snaps, near, far = assemble(received, recv_rows, blocks)

    near_swap = [(p, p ^ 1) for p in range(n_part)]
    far_swap = [(p, ((p + 1) ^ 1) - 1) for p in range(1, n_part - 1)]
    far = lax.ppermute(far, AXES, far_swap)
    near = lax.ppermute(near, AXES, near_swap)
    gram = exchange(gram_part(snaps, n_part))
    jac_snaps, reduced_tiles = apply_blocks(jac_cols.T, near, snaps, far, jac_high, jac_low, n_part)

    reduced = exchange(reduced_tiles)
    basis, jac_basis, scaled = mix(gram, snaps, jac_snaps, total_rows)
    return basis, jac_basis, finish(scaled, reduced, total_rows)


def solution(mesh):
    in_specs = (P("rows", "file"), P(), P(AXES, None, None), P(AXES, None))
    out_specs = (P(AXES, None), P(AXES, None), P())
    return jax.shard_map(shards, mesh=mesh, in_specs=in_specs, out_specs=out_specs, check_vma=False)
```

time: 132 us -> 96.4 us (0.73)
  Pallas kernels: 70.2 us -> 53.5 us
  local copies, waits for them, and re-layouts: 17.1 us -> 0.79 us
  waiting for transfers between devices: 0.01 us -> 6.65 us
  starting transfers between devices: 40.1 us -> 34.1 us
  other arithmetic: 2.57 us -> 0 us
    unnamed x14 -> x6, local copies, waits for them, and re-layouts: 11.1 us -> 0.79 us
    pallas_call x1, Pallas kernels: 27.5 us -> 20 us  [apply_blocks(): pl.pallas_call(apply_kernel, out_shape=(jax.ShapeDtypeStruct((slots, HALF...]
    all_to_all x3, waiting for transfers between devices: 0.01 us -> 6.64 us  [exchange(): return lax.all_to_all(tiles, AXES, split_axis=0, concat_axis=0, tiled=True)]
    all_to_all x3, starting transfers between devices: 34.5 us -> 30.4 us  [exchange(): return lax.all_to_all(tiles, AXES, split_axis=0, concat_axis=0, tiled=True)]
    pallas_call x3, Pallas kernels: 15.6 us -> 12.6 us  [the longest x1 6.87 us: mix(): pl.pallas_call(lambda *refs: mix_kernel(total_rows, *refs), out_shape=(ou...]
    pallas_call x1, Pallas kernels: 21.8 us -> 19 us  [split_blocks(): pl.pallas_call(split_kernel, out_shape=(out, out), grid=(slots // step,),...]
    broadcast_in_dim x4 -> x0, local copies, waits for them, and re-layouts: 2.54 us -> none  [total_over_devices(): copies = jnp.broadcast_to(block.reshape(1, 8, LANES), (n_part, 8, LANES))]
    pallas_call x1, Pallas kernels: 3.45 us -> 0.93 us  [assemble(): pl.pallas_call(assemble_kernel, out_shape=(jax.ShapeDtypeStruct((slots, H...]
  transfers between devices with their start and end apart: 5 -> 5, of which waited for: 0 -> 1; matrix products, arithmetic and copies ran while one was open for 3% -> 0% of each run, Pallas kernels for 48% -> 50%
where the time goes in v1:
time: 96.4 us; the launch traced here: 95.8 us
  Pallas kernels  53.5 us (55%)
  starting transfers between devices  34.1 us (35%)
  waiting for transfers between devices  6.65 us (7%)
    all_to_all x3, starting transfers between devices, exchange(): return lax.all_to_all(tiles, AXES, split_axis=0, concat_axis=0, tiled=True)  30.4 us
    pallas_call x1, Pallas kernels, apply_blocks(): pl.pallas_call(apply_kernel, out_shape=(jax.ShapeDtypeStruct((slots, HALF...  20 us
    pallas_call x1, Pallas kernels, split_blocks(): pl.pallas_call(split_kernel, out_shape=(out, out), grid=(slots // step,),...  19 us
    pallas_call x1, Pallas kernels, mix(): pl.pallas_call(lambda *refs: mix_kernel(total_rows, *refs), out_shape=(ou...  6.87 us
    all_to_all x3, waiting for transfers between devices, exchange(): return lax.all_to_all(tiles, AXES, split_axis=0, concat_axis=0, tiled=True)  6.64 us
    pallas_call x1, Pallas kernels, pack(): pl.pallas_call(pack_kernel, out_shape=(jax.ShapeDtypeStruct((n_part, per_...  3.74 us
    ppermute x1, starting transfers between devices, shards(): far = lax.ppermute(far, AXES, far_swap)  2.51 us
    pallas_call x1, Pallas kernels, gram_part(): pl.pallas_call(gram_kernel, out_shape=jax.ShapeDtypeStruct((n_part, 8, LA...  1.96 us
  transfers between devices with their start and end apart: 5, of which 1 were waited for; matrix products, arithmetic and copies ran while one was open for 0% of the time, Pallas kernels for 50%

profile of v1, /device:TPU:1, one launch (start us, length us, event | category | flops | bytes accessed | tf_op | source)
XLA Modules:
  0.0 95.8 jit_solution(9143272281611436523)
XLA Ops:
  0.6 3.7 %pack.1 = (f32[128,16,128]{2,1,0:T(8,128)}, s32[1,128]{1,0:T(1,128)}) custom-call(s32[128,128]{1,0:T(8,128)} %bitcast.21, f32[2048,128]{1,0:T(8,128)} %bitcast.20), custom_call_target="tpu_custom_call" | custom-call | tf_op jit(solution)/shard_map/pack/pallas_call | solution.py:103
  4.4 11.5 %all-to-all-start = ((f32[128,16,128]{2,1,0:T(8,128)}), f32[128,16,128]{2,1,0:T(8,128)S(1)}, u32[]{:S(2)}, u32[]{:S(2)}) async-start(f32[128,16,128]{2,1,0:T(8,128)} %get-tuple-element.19), calls=%async_computation | async-start | bytes 2097152 | tf_op jit(solution)/shard_map/all_to_all | solution.py:431
  15.9 0.0 copy-start.2
  15.9 0.0 copy-start.1
  15.9 19.0 %split_blocks.1 = (bf16[128,64,512]{2,1,0:T(8,128)(2,1)}, bf16[128,64,512]{2,1,0:T(8,128)(2,1)}) custom-call(f32[128,256,128]{2,1,0:T(8,128)} %bitcast.19), custom_call_target="tpu_custom_call" | custom-call | bytes 33554432 | tf_op jit(solution)/shard_map/split_blocks/pallas_call | solution.py:147
  34.9 0.0 all-to-all-done
  34.9 0.0 copy-done.2
  34.9 0.9 assemble.1
  35.8 1.2 %collective-permute-start = (f32[32,16,128]{2,1,0:T(8,128)S(1)}, f32[32,16,128]{2,1,0:T(8,128)S(1)}, u32[]{:S(2)}, u32[]{:S(2)}) collective-permute-start(f32[32,16,128]{2,1,0:T(8,128)S(1)} %get-tuple-element.24), channel_id=1, source_target_pairs={{0,1},{1,0},{2,3},{3,2},{4,5},{5,4},{6,7},{7,6},{8,9},{9,8},{10,11... | collective-permute-start | bytes 786440 | tf_op jit(solution)/shard_map/ppermute | solution.py:448
  37.1 2.5 %collective-permute-start.1 = (f32[32,16,128]{2,1,0:T(8,128)S(1)}, f32[32,16,128]{2,1,0:T(8,128)S(1)}, u32[]{:S(2)}, u32[]{:S(2)}) collective-permute-start(f32[32,16,128]{2,1,0:T(8,128)S(1)} %get-tuple-element.25), channel_id=1, source_target_pairs={{1,2},{2,1},{3,4},{4,3},{5,6},{6,5},{7,8},{8,7},{9,10},{10,9},{11,... | collective-permute-start | bytes 786440 | tf_op jit(solution)/shard_map/ppermute | solution.py:447
  39.6 2.0 %gram_part.1 = f32[128,8,128]{2,1,0:T(8,128)} custom-call(f32[128,16,128]{2,1,0:T(8,128)S(1)} %get-tuple-element.23.snap_ref.own_ref), custom_call_target="tpu_custom_call" | custom-call | flops 100663296 | bytes 3145728 | tf_op jit(solution)/shard_map/gram_part/pallas_call | solution.py:203
  41.5 9.1 %all-to-all-start.1 = ((f32[128,8,128]{2,1,0:T(8,128)}), f32[128,8,128]{2,1,0:T(8,128)S(1)}, u32[]{:S(2)}, u32[]{:S(2)}) async-start(f32[128,8,128]{2,1,0:T(8,128)} %gram_part.1), calls=%async_computation.1 | async-start | bytes 1048576 | tf_op jit(solution)/shard_map/all_to_all | solution.py:431
  50.6 0.0 collective-permute-done.near_ref
  50.6 0.0 collective-permute-done.1.far_ref
  50.7 0.0 copy-done.1
  50.7 20.0 %apply_blocks.1 = (f32[128,16,128]{2,1,0:T(8,128)S(1)}, f32[128,8,128]{2,1,0:T(8,128)S(1)}) custom-call(s32[8,128]{1,0:T(8,128)S(1)} %bitcast.18, f32[32,16,128]{2,1,0:T(8,128)S(1)} %collective-permute-done.near_ref, f32[128,16,128]{2,1,0:T(8,128)S(1)} %get-tuple-element.23.snap_ref.own_ref, f32[32,16,128]{2,1,0:T(8,128)S(1)} %collective-permute-done.1.far_ref, ...), custom_call_target="tpu_custom_call" | custom-call | flops 3221225472 | bytes 25165824 | tf_op jit(solution)/shard_map/apply_blocks/pallas_call | solution.py:312
  70.7 0.0 copy-start
  70.7 0.8 copy-done
  71.5 0.0 all-to-all-done.1.refs_0_
  71.5 9.8 %all-to-all-start.2 = ((f32[128,8,128]{2,1,0:T(8,128)}), f32[128,8,128]{2,1,0:T(8,128)S(1)}, u32[]{:S(2)}, u32[]{:S(2)}) async-start(f32[128,8,128]{2,1,0:T(8,128)} %copy-done), calls=%async_computation.2 | async-start | bytes 1048576 | tf_op jit(solution)/shard_map/all_to_all | solution.py:431
  81.3 6.9 %mix.1 = (f32[128,2048]{1,0:T(8,128)}, f32[128,2048]{1,0:T(8,128)}, f32[32,32]{1,0:T(8,128)S(1)}) custom-call(f32[128,8,128]{2,1,0:T(8,128)S(1)} %all-to-all-done.1.refs_0_, f32[2048,128]{1,0:T(8,128)S(1)} %bitcast.15, f32[2048,128]{1,0:T(8,128)S(1)} %bitcast.17), custom_call_target="tpu_custom_call" | custom-call | flops 33554432 | bytes 4194304 | tf_op jit(solution)/shard_map/mix/pallas_call | solution.py:395
  88.1 6.6 %all-to-all-done.2.refs_1_ = f32[128,8,128]{2,1,0:T(8,128)S(1)} async-done(((f32[128,8,128]{2,1,0:T(8,128)}), f32[128,8,128]{2,1,0:T(8,128)S(1)}, u32[]{:S(2)}, u32[]{:S(2)}) %all-to-all-start.2) | async-done | bytes 524320 | tf_op jit(solution)/shard_map/all_to_all | solution.py:431
  94.8 1.1 %finish.1 = f32[32,32]{1,0:T(8,128)} custom-call(f32[32,32]{1,0:T(8,128)S(1)} %get-tuple-element.31.refs_0_, f32[128,8,128]{2,1,0:T(8,128)S(1)} %all-to-all-done.2.refs_1_), custom_call_target="tpu_custom_call" | custom-call | tf_op jit(solution)/shard_map/finish/pallas_call | solution.py:420
Async XLA Ops:
  4.4 30.5 %all-to-all-start = ((f32[128,16,128]{2,1,0:T(8,128)}), f32[128,16,128]{2,1,0:T(8,128)S(1)}, u32[]{:S(2)}, u32[]{:S(2)}) async-start(f32[128,16,128]{2,1,0:T(8,128)} %get-tuple-element.19), calls=%async_computation | async-start | bytes 2097152 | tf_op jit(solution)/shard_map/all_to_all | solution.py:431
  15.9 19.0 %copy-start.2 = (s32[1,128]{1,0:T(1,128)S(1)}, s32[1,128]{1,0:T(1,128)}, u32[]{:S(2)}) copy-start(s32[1,128]{1,0:T(1,128)} %get-tuple-element.18.rows_ref) | copy-start | bytes 1540
  15.9 34.8 %copy-start.1 = (s32[128,8]{0,1:T(8,128)S(1)}, s32[128,8]{0,1:T(8,128)}, u32[]{:S(2)}) copy-start(s32[128,8]{0,1:T(8,128)} %param.7) | copy-start | bytes 12292
  35.8 14.8 %collective-permute-start = (f32[32,16,128]{2,1,0:T(8,128)S(1)}, f32[32,16,128]{2,1,0:T(8,128)S(1)}, u32[]{:S(2)}, u32[]{:S(2)}) collective-permute-start(f32[32,16,128]{2,1,0:T(8,128)S(1)} %get-tuple-element.24), channel_id=1, source_target_pairs={{0,1},{1,0},{2,3},{3,2},{4,5},{5,4},{6,7},{7,6},{8,9},{9,8},{10,11... | collective-permute-start | bytes 786440 | tf_op jit(solution)/shard_map/ppermute | solution.py:448
  37.1 13.6 %collective-permute-start.1 = (f32[32,16,128]{2,1,0:T(8,128)S(1)}, f32[32,16,128]{2,1,0:T(8,128)S(1)}, u32[]{:S(2)}, u32[]{:S(2)}) collective-permute-start(f32[32,16,128]{2,1,0:T(8,128)S(1)} %get-tuple-element.25), channel_id=1, source_target_pairs={{1,2},{2,1},{3,4},{4,3},{5,6},{6,5},{7,8},{8,7},{9,10},{10,9},{11,... | collective-permute-start | bytes 786440 | tf_op jit(solution)/shard_map/ppermute | solution.py:447
  41.5 29.9 %all-to-all-start.1 = ((f32[128,8,128]{2,1,0:T(8,128)}), f32[128,8,128]{2,1,0:T(8,128)S(1)}, u32[]{:S(2)}, u32[]{:S(2)}) async-start(f32[128,8,128]{2,1,0:T(8,128)} %gram_part.1), calls=%async_computation.1 | async-start | bytes 1048576 | tf_op jit(solution)/shard_map/all_to_all | solution.py:431
  70.7 0.8 copy-start
  71.5 23.3 %all-to-all-start.2 = ((f32[128,8,128]{2,1,0:T(8,128)}), f32[128,8,128]{2,1,0:T(8,128)S(1)}, u32[]{:S(2)}, u32[]{:S(2)}) async-start(f32[128,8,128]{2,1,0:T(8,128)} %copy-done), calls=%async_computation.2 | async-start | bytes 1048576 | tf_op jit(solution)/shard_map/all_to_all | solution.py:431

commit v2 on v1

--- a/solution.py
+++ b/solution.py
@@ -135,14 +135,14 @@
                     low_ref[s, rows, lanes] = low
         return carry
 
-    lax.fori_loop(0, jac_ref.shape[0], body, 0)
+    lax.fori_loop(0, jac_ref.shape[0], body, 0, unroll=4)
 
 
 def split_blocks(jac_blocks):
     slots = jac_blocks.shape[0]
     view = jac_blocks.reshape(slots, NNZB, BS * BS // LANES, LANES).transpose(0, 2, 1, 3)
     view = view.reshape(slots, NNZB * BS * BS // LANES, LANES)
-    step = 16
+    step = 32
     out = jax.ShapeDtypeStruct((slots, BS, NNZB * BS), jnp.bfloat16)
     return pl.pallas_call(
         split_kernel,
@@ -212,7 +212,7 @@
     )(snaps)
 
 
-CHUNK = 16
+CHUNK = 32
 
 
 def apply_kernel(cols_ref, near_ref, own_ref, far_ref, jh_hbm, jl_hbm, out_ref, copies_ref, xh_ref, xl_ref, pairs_ref, mixed_ref, jh_ref, jl_ref, sems):
@@ -297,7 +297,9 @@
         for copy in fetch(c):
             copy.wait()
         per_chunk = CHUNK // group
-        return lax.fori_loop(c * per_chunk, c * per_chunk + per_chunk, body, carry, unroll=True)
+        for j in range(per_chunk):
+            body(c * per_chunk + j, carry)
+        return carry
 
     lax.fori_loop(0, slots // CHUNK, chunk, 0)
     reduced = lax.dot_general(pairs_ref[...], mixed_ref[...], NT, precision=HIGH, preferred_element_type=jnp.float32)

time: 96.4 us -> 86.1 us (0.89)
  Pallas kernels: 53.5 us -> 41.3 us
  waiting for transfers between devices: 6.65 us -> 11.4 us
  starting transfers between devices: 34.1 us -> 31.4 us
    pallas_call x1, Pallas kernels: 20 us -> 12.4 us  [apply_blocks(): pl.pallas_call(apply_kernel, out_shape=(jax.ShapeDtypeStruct((slots, HALF...]
    all_to_all x3, waiting for transfers between devices: 6.64 us -> 11.4 us  [exchange(): return lax.all_to_all(tiles, AXES, split_axis=0, concat_axis=0, tiled=True)]
    pallas_call x1, Pallas kernels: 19 us -> 14.3 us  [split_blocks(): pl.pallas_call(split_kernel, out_shape=(out, out), grid=(slots // step,),...]
    all_to_all x3, starting transfers between devices: 30.4 us -> 28.1 us  [exchange(): return lax.all_to_all(tiles, AXES, split_axis=0, concat_axis=0, tiled=True)]
  transfers between devices with their start and end apart: 5 -> 5, of which waited for: 1 -> 3; matrix products, arithmetic and copies ran while one was open for 0% -> 0% of each run, Pallas kernels for 50% -> 42%
where the time goes in v2:
time: 86.1 us; the launch traced here: 85.7 us
  Pallas kernels  41.3 us (48%)
  starting transfers between devices  31.4 us (36%)
  waiting for transfers between devices  11.4 us (13%)
    all_to_all x3, starting transfers between devices, exchange(): return lax.all_to_all(tiles, AXES, split_axis=0, concat_axis=0, tiled=True)  28.1 us
    pallas_call x1, Pallas kernels, split_blocks(): pl.pallas_call(split_kernel, out_shape=(out, out), grid=(slots // step,),...  14.3 us
    pallas_call x1, Pallas kernels, apply_blocks(): pl.pallas_call(apply_kernel, out_shape=(jax.ShapeDtypeStruct((slots, HALF...  12.4 us
    all_to_all x3, waiting for transfers between devices, exchange(): return lax.all_to_all(tiles, AXES, split_axis=0, concat_axis=0, tiled=True)  11.4 us
    pallas_call x1, Pallas kernels, mix(): pl.pallas_call(lambda *refs: mix_kernel(total_rows, *refs), out_shape=(ou...  6.87 us
    pallas_call x1, Pallas kernels, pack(): pl.pallas_call(pack_kernel, out_shape=(jax.ShapeDtypeStruct((n_part, per_...  3.74 us
    pallas_call x1, Pallas kernels, gram_part(): pl.pallas_call(gram_kernel, out_shape=jax.ShapeDtypeStruct((n_part, 8, LA...  1.96 us
    ppermute x1, starting transfers between devices, shards(): far = lax.ppermute(far, AXES, far_swap)  1.94 us
  transfers between devices with their start and end apart: 5, of which 3 were waited for; matrix products, arithmetic and copies ran while one was open for 0% of the time, Pallas kernels for 42%

profile of v2, /device:TPU:1, one launch (start us, length us, event | category | flops | bytes accessed | tf_op | source)
XLA Modules:
  0.0 85.7 jit_solution(8138337126607252751)
XLA Ops:
  0.6 3.7 %pack.1 = (f32[128,16,128]{2,1,0:T(8,128)}, s32[1,128]{1,0:T(1,128)}) custom-call(s32[128,128]{1,0:T(8,128)} %bitcast.21, f32[2048,128]{1,0:T(8,128)} %bitcast.20), custom_call_target="tpu_custom_call" | custom-call | tf_op jit(solution)/shard_map/pack/pallas_call | solution.py:103
  4.4 11.5 %all-to-all-start = ((f32[128,16,128]{2,1,0:T(8,128)}), f32[128,16,128]{2,1,0:T(8,128)S(1)}, u32[]{:S(2)}, u32[]{:S(2)}) async-start(f32[128,16,128]{2,1,0:T(8,128)} %get-tuple-element.19), calls=%async_computation | async-start | bytes 2097152 | tf_op jit(solution)/shard_map/all_to_all | solution.py:433
  15.9 0.0 copy-start.2
  15.9 0.0 copy-start.1
  15.9 14.3 %split_blocks.1 = (bf16[128,64,512]{2,1,0:T(8,128)(2,1)}, bf16[128,64,512]{2,1,0:T(8,128)(2,1)}) custom-call(f32[128,256,128]{2,1,0:T(8,128)} %bitcast.19), custom_call_target="tpu_custom_call" | custom-call | bytes 33554432 | tf_op jit(solution)/shard_map/split_blocks/pallas_call | solution.py:147
  30.3 4.5 %all-to-all-done = f32[128,16,128]{2,1,0:T(8,128)S(1)} async-done(((f32[128,16,128]{2,1,0:T(8,128)}), f32[128,16,128]{2,1,0:T(8,128)S(1)}, u32[]{:S(2)}, u32[]{:S(2)}) %all-to-all-start) | async-done | bytes 1048608 | tf_op jit(solution)/shard_map/all_to_all | solution.py:433
  34.8 0.0 copy-done.2
  34.8 0.9 %assemble.1 = (f32[128,16,128]{2,1,0:T(8,128)S(1)}, f32[32,16,128]{2,1,0:T(8,128)S(1)}, f32[32,16,128]{2,1,0:T(8,128)S(1)}) custom-call(s32[1,128]{1,0:T(1,128)S(1)} %copy-done.2, f32[2048,128]{1,0:T(8,128)S(1)} %bitcast.16), custom_call_target="tpu_custom_call" | custom-call | tf_op jit(solution)/shard_map/assemble/pallas_call | solution.py:177
  35.7 1.3 %collective-permute-start = (f32[32,16,128]{2,1,0:T(8,128)S(1)}, f32[32,16,128]{2,1,0:T(8,128)S(1)}, u32[]{:S(2)}, u32[]{:S(2)}) collective-permute-start(f32[32,16,128]{2,1,0:T(8,128)S(1)} %get-tuple-element.24), channel_id=1, source_target_pairs={{0,1},{1,0},{2,3},{3,2},{4,5},{5,4},{6,7},{7,6},{8,9},{9,8},{10,11... | collective-permute-start | bytes 786440 | tf_op jit(solution)/shard_map/ppermute | solution.py:450
  37.1 1.9 %collective-permute-start.1 = (f32[32,16,128]{2,1,0:T(8,128)S(1)}, f32[32,16,128]{2,1,0:T(8,128)S(1)}, u32[]{:S(2)}, u32[]{:S(2)}) collective-permute-start(f32[32,16,128]{2,1,0:T(8,128)S(1)} %get-tuple-element.25), channel_id=1, source_target_pairs={{1,2},{2,1},{3,4},{4,3},{5,6},{6,5},{7,8},{8,7},{9,10},{10,9},{11,... | collective-permute-start | bytes 786440 | tf_op jit(solution)/shard_map/ppermute | solution.py:449
  39.0 2.0 %gram_part.1 = f32[128,8,128]{2,1,0:T(8,128)} custom-call(f32[128,16,128]{2,1,0:T(8,128)S(1)} %get-tuple-element.23.snap_ref.own_ref), custom_call_target="tpu_custom_call" | custom-call | flops 100663296 | bytes 3145728 | tf_op jit(solution)/shard_map/gram_part/pallas_call | solution.py:203
  41.0 7.1 %all-to-all-start.1 = ((f32[128,8,128]{2,1,0:T(8,128)}), f32[128,8,128]{2,1,0:T(8,128)S(1)}, u32[]{:S(2)}, u32[]{:S(2)}) async-start(f32[128,8,128]{2,1,0:T(8,128)} %gram_part.1), calls=%async_computation.1 | async-start | bytes 1048576 | tf_op jit(solution)/shard_map/all_to_all | solution.py:433
  48.1 0.0 collective-permute-done.near_ref
  48.1 0.0 collective-permute-done.1.far_ref
  48.1 0.0 copy-done.1
  48.2 12.4 %apply_blocks.1 = (f32[128,16,128]{2,1,0:T(8,128)S(1)}, f32[128,8,128]{2,1,0:T(8,128)S(1)}) custom-call(s32[8,128]{1,0:T(8,128)S(1)} %bitcast.18, f32[32,16,128]{2,1,0:T(8,128)S(1)} %collective-permute-done.near_ref, f32[128,16,128]{2,1,0:T(8,128)S(1)} %get-tuple-element.23.snap_ref.own_ref, f32[32,16,128]{2,1,0:T(8,128)S(1)} %collective-permute-done.1.far_ref, ...), custom_call_target="tpu_custom_call" | custom-call | flops 3221225472 | bytes 25165824 | tf_op jit(solution)/shard_map/apply_blocks/pallas_call | solution.py:314
  60.6 0.0 copy-start
  60.6 0.8 copy-done
  61.4 0.3 all-to-all-done.1.refs_0_
  61.6 9.5 %all-to-all-start.2 = ((f32[128,8,128]{2,1,0:T(8,128)}), f32[128,8,128]{2,1,0:T(8,128)S(1)}, u32[]{:S(2)}, u32[]{:S(2)}) async-start(f32[128,8,128]{2,1,0:T(8,128)} %copy-done), calls=%async_computation.2 | async-start | bytes 1048576 | tf_op jit(solution)/shard_map/all_to_all | solution.py:433
  71.1 6.9 %mix.1 = (f32[128,2048]{1,0:T(8,128)}, f32[128,2048]{1,0:T(8,128)}, f32[32,32]{1,0:T(8,128)S(1)}) custom-call(f32[128,8,128]{2,1,0:T(8,128)S(1)} %all-to-all-done.1.refs_0_, f32[2048,128]{1,0:T(8,128)S(1)} %bitcast.15, f32[2048,128]{1,0:T(8,128)S(1)} %bitcast.17), custom_call_target="tpu_custom_call" | custom-call | flops 33554432 | bytes 4194304 | tf_op jit(solution)/shard_map/mix/pallas_call | solution.py:397
  78.0 6.6 %all-to-all-done.2.refs_1_ = f32[128,8,128]{2,1,0:T(8,128)S(1)} async-done(((f32[128,8,128]{2,1,0:T(8,128)}), f32[128,8,128]{2,1,0:T(8,128)S(1)}, u32[]{:S(2)}, u32[]{:S(2)}) %all-to-all-start.2) | async-done | bytes 524320 | tf_op jit(solution)/shard_map/all_to_all | solution.py:433
  84.6 1.1 %finish.1 = f32[32,32]{1,0:T(8,128)} custom-call(f32[32,32]{1,0:T(8,128)S(1)} %get-tuple-element.31.refs_0_, f32[128,8,128]{2,1,0:T(8,128)S(1)} %all-to-all-done.2.refs_1_), custom_call_target="tpu_custom_call" | custom-call | tf_op jit(solution)/shard_map/finish/pallas_call | solution.py:422
Async XLA Ops:
  4.4 30.4 %all-to-all-start = ((f32[128,16,128]{2,1,0:T(8,128)}), f32[128,16,128]{2,1,0:T(8,128)S(1)}, u32[]{:S(2)}, u32[]{:S(2)}) async-start(f32[128,16,128]{2,1,0:T(8,128)} %get-tuple-element.19), calls=%async_computation | async-start | bytes 2097152 | tf_op jit(solution)/shard_map/all_to_all | solution.py:433
  15.9 18.9 %copy-start.2 = (s32[1,128]{1,0:T(1,128)S(1)}, s32[1,128]{1,0:T(1,128)}, u32[]{:S(2)}) copy-start(s32[1,128]{1,0:T(1,128)} %get-tuple-element.18.rows_ref) | copy-start | bytes 1540
  15.9 32.2 %copy-start.1 = (s32[128,8]{0,1:T(8,128)S(1)}, s32[128,8]{0,1:T(8,128)}, u32[]{:S(2)}) copy-start(s32[128,8]{0,1:T(8,128)} %param.7) | copy-start | bytes 12292
  35.7 12.4 %collective-permute-start = (f32[32,16,128]{2,1,0:T(8,128)S(1)}, f32[32,16,128]{2,1,0:T(8,128)S(1)}, u32[]{:S(2)}, u32[]{:S(2)}) collective-permute-start(f32[32,16,128]{2,1,0:T(8,128)S(1)} %get-tuple-element.24), channel_id=1, source_target_pairs={{0,1},{1,0},{2,3},{3,2},{4,5},{5,4},{6,7},{7,6},{8,9},{9,8},{10,11... | collective-permute-start | bytes 786440 | tf_op jit(solution)/shard_map/ppermute | solution.py:450
  37.1 11.1 %collective-permute-start.1 = (f32[32,16,128]{2,1,0:T(8,128)S(1)}, f32[32,16,128]{2,1,0:T(8,128)S(1)}, u32[]{:S(2)}, u32[]{:S(2)}) collective-permute-start(f32[32,16,128]{2,1,0:T(8,128)S(1)} %get-tuple-element.25), channel_id=1, source_target_pairs={{1,2},{2,1},{3,4},{4,3},{5,6},{6,5},{7,8},{8,7},{9,10},{10,9},{11,... | collective-permute-start | bytes 786440 | tf_op jit(solution)/shard_map/ppermute | solution.py:449
  41.0 20.7 %all-to-all-start.1 = ((f32[128,8,128]{2,1,0:T(8,128)}), f32[128,8,128]{2,1,0:T(8,128)S(1)}, u32[]{:S(2)}, u32[]{:S(2)}) async-start(f32[128,8,128]{2,1,0:T(8,128)} %gram_part.1), calls=%async_computation.1 | async-start | bytes 1048576 | tf_op jit(solution)/shard_map/all_to_all | solution.py:433
  60.6 0.8 copy-start
  61.6 23.0 %all-to-all-start.2 = ((f32[128,8,128]{2,1,0:T(8,128)}), f32[128,8,128]{2,1,0:T(8,128)S(1)}, u32[]{:S(2)}, u32[]{:S(2)}) async-start(f32[128,8,128]{2,1,0:T(8,128)} %copy-done), calls=%async_computation.2 | async-start | bytes 1048576 | tf_op jit(solution)/shard_map/all_to_all | solution.py:433

commit v3 on v2

v3 whole, which is shorter than its diff:
```python
import jax
import jax.numpy as jnp
from jax import lax
from jax.experimental import pallas as pl
from jax.experimental.pallas import tpu as pltpu
from jax.sharding import PartitionSpec as P

NSNAP = 32
BS = 64
NNZB = 8
RIM = 32
HALF = NSNAP // 2
LANES = 128
AXES = ("file", "rows")
GROUP = 4
BATCH = 8
VMEM = pltpu.VMEM
SMEM = pltpu.SMEM
NT = (((1,), (1,)), ((), ()))
HIGH = lax.Precision.HIGHEST


def spec(space):
    return pl.BlockSpec(memory_space=space)


def limit(mib):
    return pltpu.CompilerParams(vmem_limit_bytes=mib * 1024 * 1024)


def cost(flops, nbytes):
    return pl.CostEstimate(flops=flops, bytes_accessed=nbytes, transcendentals=0)


def low_half(shape):
    return lax.broadcasted_iota(jnp.int32, shape, len(shape) - 1) < BS


def split_pair(first, second):
    low = low_half(first.shape)
    zero = jnp.where(low, first, pltpu.roll(second, BS, 1))
    one = jnp.where(low, pltpu.roll(first, BS, 1), second)
    return zero, one


def to_tile(block):
    return jnp.concatenate([block[8 * i : 8 * i + 8, 0:NSNAP] for i in range(4)], axis=1)


def tree_sum(parts):
    while len(parts) > 1:
        parts = [x + y for x, y in zip(parts[0::2], parts[1::2])]
    return parts[0]


def from_tile(tile):
    return [tile] + [pltpu.roll(tile, LANES - NSNAP * i, 1) for i in range(1, 4)]


def my_part():
    return lax.axis_index("file") * lax.axis_size("rows") + lax.axis_index("rows")


def pack_kernel(map_ref, cols_ref, snap_hbm, out_ref, recv_ref, snap_ref, index_ref, rows_ref, snap_sem, rows_sem):
    fetch = pltpu.make_async_copy(snap_hbm, snap_ref, snap_sem)
    fetch.start()
    n_part, slots = map_ref.shape
    per_pair = out_ref.shape[1] // 4
    held = slots * per_pair

    local = map_ref[...] - lax.axis_index("rows") * held
    group = local >> 7
    within = (local & 127).astype(jnp.float32)
    ones = jnp.ones((8, slots), jnp.bfloat16)
    for q in range(per_pair):
        part = jnp.where(group == q, within, 0.0).astype(jnp.bfloat16)
        found = lax.dot_general(ones, part, NT, preferred_element_type=jnp.float32)
        row = found[0:1].astype(jnp.int32) + q * slots
        index_ref[q : q + 1, :] = (row >> 3) * 32 + (row & 7)
    move = pltpu.make_async_copy(index_ref, rows_ref, rows_sem)
    move.start()

    mine = map_ref[pl.ds(my_part(), 1), :]
    recv_ref[0:1, :] = (mine >> 9) * (4 * per_pair) + ((mine >> 7) & (per_pair - 1)) * 4

    cols = cols_ref[...]
    start = my_part() * slots
    below = ((cols >= 0) & (cols < start)).astype(jnp.int32)
    above = (cols >= start + slots).astype(jnp.int32)
    uses_far = jnp.where(my_part() % 2 == 1, above, below)
    recv_ref[1:2, :] = jnp.max(uses_far, axis=0, keepdims=True)
    move.wait()
    fetch.wait()

    def body(part, carry):
        for q in range(per_pair):
            row = rows_ref[q, part]
            out_ref[part, 4 * q : 4 * q + 4, :] = snap_ref[pl.ds(row, 4, stride=8), :]
        return carry

    lax.fori_loop(0, n_part, body, 0, unroll=8)


def pack(snapshots, part_map, cols, n_part):
    blocks, width = snapshots.shape
    tiles = width // LANES
    slots = part_map.shape[0] // n_part
    per_pair = blocks // slots
    assert slots == 128 and tiles == 4 and per_pair == 4
    view = snapshots.reshape(blocks // 8, 8, tiles, LANES).transpose(0, 2, 1, 3)
    view = view.reshape(blocks * tiles, LANES)
    return pl.pallas_call(
        pack_kernel,
        out_shape=(
            jax.ShapeDtypeStruct((n_part, per_pair * tiles, LANES), jnp.float32),
            jax.ShapeDtypeStruct((2, slots), jnp.int32),
        ),
        in_specs=[spec(VMEM), spec(VMEM), spec(pl.ANY)],
        out_specs=(spec(VMEM), spec(VMEM)),
        scratch_shapes=[
            pltpu.VMEM(view.shape, jnp.float32),
            pltpu.VMEM((per_pair, n_part), jnp.int32),
            pltpu.SMEM((per_pair, n_part), jnp.int32),
            pltpu.SemaphoreType.DMA,
            pltpu.SemaphoreType.DMA,
        ],
        compiler_params=limit(60),
        name="pack",
    )(part_map.reshape(n_part, slots), cols, view)


def order_groups(flags_ref, order_ref):
    count = order_ref.shape[0] - 1

    def body(g, found):
        at = g * GROUP
        far = flags_ref[1, at]
        for i in range(1, GROUP):
            far = far | flags_ref[1, at + i]
        order_ref[jnp.where(far == 1, count - 1 - (g - found), found)] = g
        return found + 1 - far

    order_ref[count] = lax.fori_loop(0, count, body, jnp.int32(0)) // BATCH


def split_kernel(flags_ref, jac_ref, out_ref, order_ref):
    @pl.when(pl.program_id(0) == 0)
    def _():
        order_groups(flags_ref, order_ref)

    def body(s, carry):
        for pair in range(NNZB // 2):
            for tb in range(2):
                first = jac_ref[s, pl.ds(tb * 128 + 2 * pair, 16, stride=8), :]
                second = jac_ref[s, pl.ds(tb * 128 + 2 * pair + 1, 16, stride=8), :]
                for r2, part in enumerate(split_pair(first, second)):
                    high = part.astype(jnp.bfloat16)
                    low = (part - high.astype(jnp.float32)).astype(jnp.bfloat16)
                    rows = slice(32 * r2 + 16 * tb, 32 * r2 + 16 * tb + 16)
                    lanes = slice(LANES * pair, LANES * pair + LANES)
                    out_ref[s, 0, rows, lanes] = high
                    out_ref[s, 1, rows, lanes] = low
        return carry

    lax.fori_loop(0, jac_ref.shape[0], body, 0, unroll=4)


def split_blocks(jac_blocks, flags):
    slots = jac_blocks.shape[0]
    view = jac_blocks.reshape(slots, NNZB, BS * BS // LANES, LANES).transpose(0, 2, 1, 3)
    view = view.reshape(slots, NNZB * BS * BS // LANES, LANES)
    step = 32
    out = jax.ShapeDtypeStruct((slots, 2, BS, NNZB * BS), jnp.bfloat16)
    return pl.pallas_call(
        split_kernel,
        out_shape=(out, jax.ShapeDtypeStruct((slots // GROUP + 1,), jnp.int32)),
        grid=(slots // step,),
        in_specs=[spec(SMEM), pl.BlockSpec((step,) + view.shape[1:], lambda i: (i, 0, 0))],
        out_specs=(pl.BlockSpec((step,) + out.shape[1:], lambda i: (i, 0, 0, 0)), spec(SMEM)),
        compiler_params=limit(48),
        cost_estimate=cost(0, 32 * 1024 * 1024),
        name="split_blocks",
    )(flags, view)


def assemble_kernel(rows_ref, recv_ref, snap_ref, near_ref, far_ref):
    slots = snap_ref.shape[0]
    per_file = recv_ref.shape[0] // 4

    def body(s, carry):
        row = rows_ref[0, s]
        for f in range(4):
            snap_ref[s, 4 * f : 4 * f + 4, :] = recv_ref[pl.ds(f * per_file + row, 4), :]
        return carry

    lax.fori_loop(0, slots, body, 0, unroll=8)
    odd = my_part() % 2
    near_ref[...] = snap_ref[pl.ds((1 - odd) * (slots - RIM), RIM)]
    far_ref[...] = snap_ref[pl.ds(odd * (slots - RIM), RIM)]


def assemble(received, rows, slots):
    rim = jax.ShapeDtypeStruct((RIM, HALF, LANES), jnp.float32)
    return pl.pallas_call(
        assemble_kernel,
        out_shape=(jax.ShapeDtypeStruct((slots, HALF, LANES), jnp.float32), rim, rim),
        in_specs=[spec(SMEM), spec(VMEM)],
        out_specs=(spec(VMEM),) * 3,
        compiler_params=limit(6),
        name="assemble",
    )(rows, received.reshape(-1, LANES))


def make_pairs(snap_ref, pairs_ref):
    for sp in range(snap_ref.shape[0] // 2):
        zero, one = split_pair(snap_ref[2 * sp], snap_ref[2 * sp + 1])
        pairs_ref[0:HALF, sp * LANES : sp * LANES + LANES] = zero
        pairs_ref[HALF:NSNAP, sp * LANES : sp * LANES + LANES] = one


def gram_kernel(snap_ref, tile_ref, pairs_ref):
    make_pairs(snap_ref, pairs_ref)
    pairs = pairs_ref[...]
    gram = lax.dot_general(pairs, pairs, NT, precision=HIGH, preferred_element_type=jnp.float32)
    tile_ref[...] = to_tile(gram)


def gram_part(snaps):
    slots = snaps.shape[0]
    return pl.pallas_call(
        gram_kernel,
        out_shape=jax.ShapeDtypeStruct((8, LANES), jnp.float32),
        in_specs=[spec(VMEM)],
        out_specs=spec(VMEM),
        scratch_shapes=[pltpu.VMEM((NSNAP, slots * BS), jnp.float32)],
        compiler_params=limit(8),
        cost_estimate=cost(2 * 6 * NSNAP * NSNAP * slots * BS, 3 * 1024 * 1024),
        name="gram_part",
    )(snaps)


def fill(ref, xh_ref, xl_ref, base):
    low = low_half((HALF, LANES))

    def body(s, carry):
        x = ref[s]
        y = pltpu.roll(x, BS, 1)
        for kk, part in enumerate((jnp.where(low, x, y), jnp.where(low, y, x))):
            high = part.astype(jnp.bfloat16)
            rest = (part - high.astype(jnp.float32)).astype(jnp.bfloat16)
            xh_ref[base + s, HALF * kk : HALF * kk + HALF, :] = high
            xl_ref[base + s, HALF * kk : HALF * kk + HALF, :] = rest
        return carry

    lax.fori_loop(0, ref.shape[0], body, 0, unroll=8)


def run_batches(first, last, cols_ref, own_ref, jac_hbm, out_ref, red_ref, xh_ref, xl_ref, jac_ref, order_ref, sems, prepare):
    slots = own_ref.shape[0]
    low32 = low_half((NSNAP, LANES))
    lane = lax.broadcasted_iota(jnp.int32, (NSNAP, LANES), 1)
    r = lane % BS
    lanes = lane - r + (r % 2) * (BS // 2) + r // 2
    first_slot = my_part() * slots - RIM
    last_row = slots + 2 * RIM - 1

    def fetch(at):
        source = pl.ds(order_ref[at] * GROUP, GROUP)
        target = pl.ds(at * GROUP, GROUP)
        return pltpu.make_async_copy(jac_hbm.at[source], jac_ref.at[target], sems.at[at])

    def start(at, carry):
        fetch(at).start()
        return carry

    lax.fori_loop(first * BATCH, last * BATCH, start, 0)
    prepare()

    def table_row(n, s):
        column = cols_ref[n, s]
        row = jnp.minimum(jnp.maximum(column - first_slot, 0), last_row)
        return jnp.where(column < 0, last_row + 1, row)

    def product(at):
        g = order_ref[at]
        highs, lows = [], []
        for i in range(GROUP):
            hi_parts, lo_parts = [], []
            for pair in range(NNZB // 2):
                a = table_row(2 * pair, g * GROUP + i)
                b = table_row(2 * pair + 1, g * GROUP + i)
                hi_parts.append(jnp.where(low32, xh_ref[a], xh_ref[b]))
                lo_parts.append(jnp.where(low32, xl_ref[a], xl_ref[b]))
            highs.append(jnp.concatenate(hi_parts, axis=1))
            lows.append(jnp.concatenate(lo_parts, axis=1))
        high = jnp.concatenate(highs, axis=0)
        both = jnp.concatenate(highs + lows, axis=0)
        rows = pl.ds(at * GROUP, GROUP)
        jh = jac_ref[rows, 0].reshape(GROUP * BS, NNZB * BS)
        jl = jac_ref[rows, 1].reshape(GROUP * BS, NNZB * BS)
        big = lax.dot_general(both, jh, NT, preferred_element_type=jnp.float32)
        acc = big[0 : GROUP * NSNAP] + big[GROUP * NSNAP :]
        acc = acc + lax.dot_general(high, jl, NT, preferred_element_type=jnp.float32)
        results, pairs = [], []
        for ip in range(GROUP // 2):
            tile = acc[:, LANES * ip : LANES * ip + LANES]
            top = tile[2 * ip * NSNAP : 2 * ip * NSNAP + NSNAP]
            bottom = tile[2 * ip * NSNAP + NSNAP : 2 * ip * NSNAP + 2 * NSNAP]
            mixed = jnp.take_along_axis(jnp.where(low32, top, bottom), lanes, axis=1)
            s = g * GROUP + 2 * ip
            out_ref[s], out_ref[s + 1] = split_pair(mixed[0:HALF], mixed[HALF:NSNAP])
            results.append(mixed)
            pairs.append(jnp.concatenate(split_pair(own_ref[s], own_ref[s + 1]), axis=0))
        return pairs, results

    red_ref[...] = jnp.zeros_like(red_ref)

    def batch(b, carry):
        for j in range(BATCH):
            fetch(b * BATCH + j).wait()
        pairs, results = [], []
        for j in range(BATCH):
            x, y = product(b * BATCH + j)
            pairs += x
            results += y
        red_ref[...] += lax.dot_general(
            jnp.concatenate(pairs, axis=1),
            jnp.concatenate(results, axis=1),
            NT,
            precision=HIGH,
            preferred_element_type=jnp.float32,
        )
        return carry

    lax.fori_loop(first, last, batch, 0)


def fill_zero(xh_ref, xl_ref):
    xh_ref[xh_ref.shape[0] - 1] = jnp.zeros(xh_ref.shape[1:], jnp.bfloat16)
    xl_ref[xl_ref.shape[0] - 1] = jnp.zeros(xl_ref.shape[1:], jnp.bfloat16)


def near_kernel(order_ref, cols_ref, near_ref, own_ref, jac_hbm, out_ref, red_ref, xh_ref, xl_ref, jac_ref, sems):
    slots = own_ref.shape[0]
    odd = my_part() % 2

    def prepare():
        fill(near_ref, xh_ref, xl_ref, (1 - odd) * (slots + RIM))
        fill(own_ref, xh_ref, xl_ref, RIM)
        fill_zero(xh_ref, xl_ref)

    batches = order_ref[slots // GROUP]
    run_batches(0, batches, cols_ref, own_ref, jac_hbm, out_ref, red_ref, xh_ref, xl_ref, jac_ref, order_ref, sems, prepare)


def far_kernel(order_ref, cols_ref, near_ref, far_ref, own_ref, gram_ref, done_ref, red_in_ref, jac_hbm, out_ref, keep_ref, give_ref, red_ref, xh_ref, xl_ref, jac_ref, sems):
    slots = own_ref.shape[0]
    odd = my_part() % 2

    def prepare():
        out_ref[...] = done_ref[...]
        fill(near_ref, xh_ref, xl_ref, (1 - odd) * (slots + RIM))
        fill(own_ref, xh_ref, xl_ref, RIM)
        fill(far_ref, xh_ref, xl_ref, odd * (slots + RIM))
        fill_zero(xh_ref, xl_ref)

    batches = order_ref[slots // GROUP]
    last = slots // GROUP // BATCH
    run_batches(batches, last, cols_ref, own_ref, jac_hbm, out_ref, red_ref, xh_ref, xl_ref, jac_ref, order_ref, sems, prepare)

    gram = gram_ref[...]
    reduced = to_tile(red_in_ref[...] + red_ref[...])
    keep_ref[...] = jnp.where(odd == 1, reduced, gram)
    give_ref[...] = jnp.where(odd == 1, gram, reduced)


def scratch(slots, jac_split):
    table = pltpu.VMEM((slots + 2 * RIM + 1, NSNAP, LANES), jnp.bfloat16)
    return [table, table, pltpu.VMEM(jac_split.shape, jac_split.dtype), pltpu.SemaphoreType.DMA((slots // GROUP,))]


def apply_near(order, cols, near, own, jac_split):
    slots = own.shape[0]
    return pl.pallas_call(
        near_kernel,
        out_shape=(
            jax.ShapeDtypeStruct((slots, HALF, LANES), jnp.float32),
            jax.ShapeDtypeStruct((NSNAP, NSNAP), jnp.float32),
        ),
        in_specs=[spec(SMEM)] * 2 + [spec(VMEM)] * 2 + [spec(pl.ANY)],
        out_specs=(spec(VMEM),) * 2,
        scratch_shapes=scratch(slots, jac_split),
        compiler_params=limit(50),
        cost_estimate=cost(2 * 3 * slots * 3 * NSNAP * 512 * BS, 20 * 1024 * 1024),
        name="apply_near",
    )(order, cols, near, own, jac_split)


def apply_far(order, cols, near, far, own, gram, done, jac_split):
    slots = own.shape[0]
    tile = jax.ShapeDtypeStruct((8, LANES), jnp.float32)
    return pl.pallas_call(
        far_kernel,
        out_shape=(jax.ShapeDtypeStruct((slots, HALF, LANES), jnp.float32), tile, tile),
        in_specs=[spec(SMEM)] * 2 + [spec(VMEM)] * 6 + [spec(pl.ANY)],
        out_specs=(spec(VMEM),) * 3,
        scratch_shapes=[pltpu.VMEM((NSNAP, NSNAP), jnp.float32)] + scratch(slots, jac_split),
        compiler_params=limit(50),
        cost_estimate=cost(2 * 3 * slots * NSNAP * 512 * BS, 8 * 1024 * 1024),
        name="apply_far",
    )(order, cols, near, far, own, gram, *done, jac_split)


def factor(gram, total_rows):
    groups = range(NSNAP // 8)
    row = lax.broadcasted_iota(jnp.int32, (8, LANES), 0)
    lane = lax.broadcasted_iota(jnp.int32, (8, LANES), 1)
    rank = [2 * ((row + 8 * v) % HALF) + (row + 8 * v) // HALF for v in groups]
    work = [
        jnp.where(lane < NSNAP, gram[v], jnp.where(lane - NSNAP == row + 8 * v, 1.0, 0.0).astype(jnp.float32))
        for v in groups
    ]
    row_of = lambda x, p: jnp.broadcast_to(x[p // 8][p % 8 : p % 8 + 1, :], (8, LANES))
    step = 4
    for first in range(0, NSNAP, step):
        at = [(k % 2) * HALF + k // 2 for k in range(first, first + step)]
        rows = [row_of(work, p) for p in at]
        cols = [[jnp.broadcast_to(x[:, p : p + 1], (8, LANES)) for x in work] for p in at]
        block = [[row_of(cols[n], at[m]) for n in range(step)] for m in range(step)]
        below = [jnp.zeros((8, LANES), jnp.float32) for _ in groups]
        for m in range(step):
            inverse = 1.0 / block[m][m]
            for v in groups:
                ratio = cols[m][v] * inverse
                below[v] = below[v] + ratio * rows[m]
                for n in range(m + 1, step):
                    cols[n][v] = cols[n][v] - ratio * block[m][n]
            for n in range(m + 1, step):
                ratio = block[n][m] * inverse
                rows[n] = rows[n] - ratio * rows[m]
                block[n] = [x - ratio * y for x, y in zip(block[n], block[m])]
        for v in groups:
            new = jnp.where(rank[v] >= first + step, work[v] - below[v], work[v])
            for m in range(step):
                if at[m] // 8 == v:
                    new = jnp.where(row == at[m] % 8, rows[m], new)
            work[v] = new
    scaled = []
    for v in groups:
        diag = jnp.sum(jnp.where(lane == row + 8 * v, work[v], 0.0), axis=1, keepdims=True)
        scaled.append(pltpu.roll(work[v], LANES - NSNAP, 1) * (float(total_rows) ** 0.5 / jnp.sqrt(diag)))
    return jnp.concatenate(scaled, axis=0)


def finish(scaled, reduced):
    row = lax.broadcasted_iota(jnp.int32, (NSNAP, NSNAP), 0)
    col = lax.broadcasted_iota(jnp.int32, (NSNAP, NSNAP), 1)
    place = jnp.where(col == (row % 2) * HALF + row // 2, 1.0, 0.0).astype(jnp.float32)
    dot = lambda a, b, dims: lax.dot_general(a, b, dims, precision=HIGH, preferred_element_type=jnp.float32)
    nn = (((1,), (0,)), ((), ()))
    natural = dot(place, scaled, nn)
    return dot(dot(natural, reduced, nn), natural, NT)


def mix_kernel(total_rows, sums_ref, snap_ref, jac_ref, basis_ref, out_ref, final_ref, same_ref, swap_ref, plain_ref, turned_ref):
    low = low_half((HALF, LANES))

    @pl.when(pl.program_id(0) == 0)
    def _():
        n_part = sums_ref.shape[0]
        gram = tree_sum([sums_ref[p] for p in range(0, n_part, 2)])
        scaled = factor(from_tile(gram), total_rows)
        reduced = tree_sum([sums_ref[p] for p in range(1, n_part, 2)])
        reduced = jnp.concatenate(from_tile(reduced), axis=0)[:, 0:NSNAP]
        final_ref[...] = finish(scaled[:, 0:NSNAP], reduced) / float(total_rows)
        wide = lambda kk, j: jnp.broadcast_to(scaled[kk * HALF : kk * HALF + HALF, j : j + 1], (HALF, LANES))
        for j2 in range(HALF):
            same_ref[j2] = jnp.where(low, wide(0, j2), wide(1, HALF + j2))
            swap_ref[j2] = jnp.where(low, wide(0, HALF + j2), wide(1, j2))

    both = range(2)
    for source, target in ((snap_ref, basis_ref), (jac_ref, out_ref)):
        def body(pair, carry):
            for j2 in range(HALF):
                for h in both:
                    x = source[pl.ds((2 * pair + h) * 8 * HALF + j2, 8, stride=HALF), :]
                    plain_ref[h, j2] = x
                    turned_ref[h, j2] = pltpu.roll(x, BS, 1)
            for k4 in range(0, HALF, 4):
                totals = {}
                for j2 in range(k4 + 4):
                    values = [(plain_ref[h, j2], turned_ref[h, j2]) for h in both]
                    for k2 in range(max(k4, j2), k4 + 4):
                        same = jnp.broadcast_to(same_ref[j2, k2 : k2 + 1, :], (8, LANES))
                        swap = jnp.broadcast_to(swap_ref[j2, k2 : k2 + 1, :], (8, LANES))
                        for h in both:
                            term = same * values[h][0] + swap * values[h][1]
                            totals[k2, h] = totals[k2, h] + term if j2 else term
                for k2 in range(k4, k4 + 4):
                    for h in both:
                        rows = pl.ds(pl.multiple_of((2 * pair + h) * 8, 8), 8)
                        target[rows, LANES * k2 : LANES * k2 + LANES] = totals[k2, h]
            return carry

        lax.fori_loop(0, target.shape[0] // 16, body, 0)


def mix(sums, snaps, jac, total_rows):
    slots = snaps.shape[0]
    step = 32
    out = jax.ShapeDtypeStruct((slots, NSNAP * BS), jnp.float32)
    flat = lambda x: x.reshape(slots * HALF, LANES)
    rows = pl.BlockSpec((step * HALF, LANES), lambda i: (i, 0))
    return pl.pallas_call(
        lambda *refs: mix_kernel(total_rows, *refs),
        out_shape=(out, out, jax.ShapeDtypeStruct((NSNAP, NSNAP), jnp.float32)),
        grid=(slots // step,),
        in_specs=[pl.BlockSpec(sums.shape, lambda i: (0, 0, 0)), rows, rows],
        out_specs=[pl.BlockSpec((step, NSNAP * BS), lambda i: (i, 0))] * 2 + [pl.BlockSpec((NSNAP, NSNAP), lambda i: (0, 0))],
        scratch_shapes=[pltpu.VMEM((HALF, HALF, LANES), jnp.float32)] * 2 + [pltpu.VMEM((2, HALF, 8, LANES), jnp.float32)] * 2,
        cost_estimate=cost(2 * 2 * slots * BS * NSNAP * NSNAP, 4 * 1024 * 1024),
        compiler_params=limit(12),
        name="mix",
    )(sums, flat(snaps), flat(jac))


def exchange(tiles):
    return lax.all_to_all(tiles, AXES, split_axis=0, concat_axis=0, tiled=True)


def shards(snapshots, part_map, jac_blocks, jac_cols):
    n_part = lax.axis_size("file") * lax.axis_size("rows")
    blocks = jac_blocks.shape[0]
    total_rows = blocks * BS * n_part

    cols = jac_cols.T
    packed, table = pack(snapshots, part_map, cols, n_part)
    received = exchange(packed)
    jac_split, order = split_blocks(jac_blocks, table)
    received, jac_split, order = lax.optimization_barrier((received, jac_split, order))
    snaps, near, far = assemble(received, table, blocks)

    near_swap = [(p, p ^ 1) for p in range(n_part)]
    far_swap = [(p, ((p + 1) ^ 1) - 1) for p in range(1, n_part - 1)]
    far = lax.ppermute(far, AXES, far_swap)
    near = lax.ppermute(near, AXES, near_swap)
    gram = gram_part(snaps)
    done = apply_near(order, cols, near, snaps, jac_split)
    done, far = lax.optimization_barrier((done, far))
    jac_snaps, keep, give = apply_far(order, cols, near, far, snaps, gram, done, jac_split)
    pair_sum = keep + lax.ppermute(give, AXES, near_swap)
    sums = exchange(jnp.broadcast_to(pair_sum[None], (n_part, 8, LANES)))
    return mix(sums, snaps, jac_snaps, total_rows)


def solution(mesh):
    in_specs = (P("rows", "file"), P(), P(AXES, None, None), P(AXES, None))
    out_specs = (P(AXES, None), P(AXES, None), P())
    return jax.shard_map(shards, mesh=mesh, in_specs=in_specs, out_specs=out_specs, check_vma=False)
```

time: 86.1 us -> 83.4 us (0.969)
  blocking collectives: 0 us -> 20.5 us
  starting transfers between devices: 31.4 us -> 14.9 us
  waiting for transfers between devices: 11.4 us -> 4.4 us
    all_to_all x0 -> x1, blocking collectives: none -> 20.5 us  [exchange(): return lax.all_to_all(tiles, AXES, split_axis=0, concat_axis=0, tiled=True)]
    all_to_all x3 -> x1, starting transfers between devices: 28.1 us -> 11.5 us  [exchange(): return lax.all_to_all(tiles, AXES, split_axis=0, concat_axis=0, tiled=True)]
    all_to_all x3 -> x1, waiting for transfers between devices: 11.4 us -> 3.24 us  [exchange(): return lax.all_to_all(tiles, AXES, split_axis=0, concat_axis=0, tiled=True)]
    pallas_call x4, Pallas kernels: 29.8 us -> 31.1 us  [the longest x1 15 us: split_blocks(): pl.pallas_call(split_kernel, out_shape=(out, jax.ShapeDtypeStruct((slots...]
    ppermute x0 -> x1, waiting for transfers between devices: none -> 1.15 us  [shards(): pair_sum = keep + lax.ppermute(give, AXES, near_swap)]
  transfers between devices with their start and end apart: 5 -> 4, of which waited for: 3 -> 2; matrix products, arithmetic and copies ran while one was open for 0% -> 0% of each run, Pallas kernels for 42% -> 31%
where the time goes in v3:
time: 83.4 us; the launch traced here: 83.1 us
  Pallas kernels  41.8 us (50%)
  blocking collectives  20.5 us (25%)
  starting transfers between devices  14.9 us (18%)
  waiting for transfers between devices  4.4 us (5%)
    all_to_all x1, blocking collectives, exchange(): return lax.all_to_all(tiles, AXES, split_axis=0, concat_axis=0, tiled=True)  20.5 us
    pallas_call x1, Pallas kernels, split_blocks(): pl.pallas_call(split_kernel, out_shape=(out, jax.ShapeDtypeStruct((slots...  15 us
    all_to_all x1, starting transfers between devices, exchange(): return lax.all_to_all(tiles, AXES, split_axis=0, concat_axis=0, tiled=True)  11.5 us
    pallas_call x1, Pallas kernels, apply_near(): pl.pallas_call(near_kernel, out_shape=(jax.ShapeDtypeStruct((slots, HALF,...  9.6 us
    pallas_call x1, Pallas kernels, mix(): pl.pallas_call(lambda *refs: mix_kernel(total_rows, *refs), out_shape=(ou...  6.02 us
    pallas_call x1, Pallas kernels, apply_far(): pl.pallas_call(far_kernel, out_shape=(jax.ShapeDtypeStruct((slots, HALF,...  5.44 us
    pallas_call x1, Pallas kernels, pack(): pl.pallas_call(pack_kernel, out_shape=(jax.ShapeDtypeStruct((n_part, per_...  3.76 us
    all_to_all x1, waiting for transfers between devices, exchange(): return lax.all_to_all(tiles, AXES, split_axis=0, concat_axis=0, tiled=True)  3.24 us
  transfers between devices with their start and end apart: 4, of which 2 were waited for; matrix products, arithmetic and copies ran while one was open for 0% of the time, Pallas kernels for 31%

profile of v3, /device:TPU:1, one launch (start us, length us, event | category | flops | bytes accessed | tf_op | source)
XLA Modules:
  0.0 83.1 jit_solution(15688953085358920522)
XLA Ops:
  0.6 0.0 copy-start
  0.6 3.8 %pack.1 = (f32[128,16,128]{2,1,0:T(8,128)}, s32[2,128]{1,0:T(2,128)}) custom-call(s32[128,128]{1,0:T(8,128)} %bitcast.23, s32[8,128]{1,0:T(8,128)} %bitcast.18, f32[2048,128]{1,0:T(8,128)} %bitcast.22), custom_call_target="tpu_custom_call" | custom-call | tf_op jit(solution)/shard_map/pack/pallas_call | solution.py:112
  4.4 0.0 copy-start.2
  4.4 11.5 %all-to-all-start = ((f32[128,16,128]{2,1,0:T(8,128)}), f32[128,16,128]{2,1,0:T(8,128)S(1)}, u32[]{:S(2)}, u32[]{:S(2)}) async-start(f32[128,16,128]{2,1,0:T(8,128)} %get-tuple-element.21), calls=%async_computation | async-start | bytes 2097152 | tf_op jit(solution)/shard_map/all_to_all | solution.py:528
  15.9 0.0 copy-start.1
  15.9 0.7 copy-done.1
  16.6 15.0 %split_blocks.1 = (bf16[128,2,64,512]{3,2,1,0:T(8,128)(2,1)}, s32[33]{0:T(128)S(1)}) custom-call(s32[2,128]{1,0:T(2,128)S(1)} %copy-done.1, f32[128,256,128]{2,1,0:T(8,128)} %bitcast.21), custom_call_target="tpu_custom_call" | custom-call | bytes 33554432 | tf_op jit(solution)/shard_map/split_blocks/pallas_call | solution.py:174
  31.6 3.2 %all-to-all-done = f32[128,16,128]{2,1,0:T(8,128)S(1)} async-done(((f32[128,16,128]{2,1,0:T(8,128)}), f32[128,16,128]{2,1,0:T(8,128)S(1)}, u32[]{:S(2)}, u32[]{:S(2)}) %all-to-all-start) | async-done | bytes 1048608 | tf_op jit(solution)/shard_map/all_to_all | solution.py:528
  34.8 0.0 copy-done.2
  34.8 0.9 %assemble.1 = (f32[128,16,128]{2,1,0:T(8,128)S(1)}, f32[32,16,128]{2,1,0:T(8,128)S(1)}, f32[32,16,128]{2,1,0:T(8,128)S(1)}) custom-call(s32[2,128]{1,0:T(2,128)S(1)} %copy-done.2, f32[2048,128]{1,0:T(8,128)S(1)} %bitcast.16), custom_call_target="tpu_custom_call" | custom-call | tf_op jit(solution)/shard_map/assemble/pallas_call | solution.py:204
  35.8 1.3 %collective-permute-start = (f32[32,16,128]{2,1,0:T(8,128)S(1)}, f32[32,16,128]{2,1,0:T(8,128)S(1)}, u32[]{:S(2)}, u32[]{:S(2)}) collective-permute-start(f32[32,16,128]{2,1,0:T(8,128)S(1)} %get-tuple-element.27), channel_id=1, source_target_pairs={{0,1},{1,0},{2,3},{3,2},{4,5},{5,4},{6,7},{7,6},{8,9},{9,8},{10,11... | collective-permute-start | bytes 786440 | tf_op jit(solution)/shard_map/ppermute | solution.py:546
  37.1 1.9 %collective-permute-start.1 = (f32[32,16,128]{2,1,0:T(8,128)S(1)}, f32[32,16,128]{2,1,0:T(8,128)S(1)}, u32[]{:S(2)}, u32[]{:S(2)}) collective-permute-start(f32[32,16,128]{2,1,0:T(8,128)S(1)} %get-tuple-element.32), channel_id=1, source_target_pairs={{1,2},{2,1},{3,4},{4,3},{5,6},{6,5},{7,8},{8,7},{9,10},{10,9},{11,... | collective-permute-start | bytes 786440 | tf_op jit(solution)/shard_map/ppermute | solution.py:545
  39.1 1.1 %gram_part.1.gram_ref = f32[8,128]{1,0:T(8,128)S(1)} custom-call(f32[128,16,128]{2,1,0:T(8,128)S(1)} %get-tuple-element.28.own_ref.snap_ref), custom_call_target="tpu_custom_call" | custom-call | flops 100663296 | bytes 3145728 | tf_op jit(solution)/shard_map/gram_part/pallas_call | solution.py:230
  40.2 0.0 collective-permute-done.near_ref
  40.2 0.0 copy-done
  40.2 9.6 %apply_near.1 = (f32[128,16,128]{2,1,0:T(8,128)S(1)}, f32[32,32]{1,0:T(8,128)S(1)}) custom-call(s32[33]{0:T(128)S(1)} %get-tuple-element.25.order_ref, s32[8,128]{1,0:T(8,128)S(1)} %bitcast.19, f32[32,16,128]{2,1,0:T(8,128)S(1)} %collective-permute-done.near_ref, f32[128,16,128]{2,1,0:T(8,128)S(1)} %get-tuple-element.28.own_ref.snap_ref, ...), custom_call_target="tpu_custom_call" | custom-call | flops 2415919104 | bytes 20971520 | tf_op jit(solution)/shard_map/apply_near/pallas_call | solution.py:384
  49.8 0.0 collective-permute-done.1.far_ref
  49.8 5.4 %apply_far.1 = (f32[128,16,128]{2,1,0:T(8,128)S(1)}, f32[8,128]{1,0:T(8,128)S(1)}, f32[8,128]{1,0:T(8,128)S(1)}) custom-call(s32[33]{0:T(128)S(1)} %get-tuple-element.25.order_ref, s32[8,128]{1,0:T(8,128)S(1)} %bitcast.20, f32[32,16,128]{2,1,0:T(8,128)S(1)} %collective-permute-done.near_ref, f32[32,16,128]{2,1,0:T(8,128)S(1)} %collective-permute-done.1.far_ref, ...), custom_call_target="tpu_custom_call" | custom-call | flops 805306368 | bytes 8388608 | tf_op jit(solution)/shard_map/apply_far/pallas_call | solution.py:402
  55.3 0.1 collective-permute-start.2
  55.3 1.2 %collective-permute-done.2 = f32[8,128]{1,0:T(8,128)S(1)} collective-permute-done((f32[8,128]{1,0:T(8,128)S(1)}, f32[8,128]{1,0:T(8,128)S(1)}, u32[]{:S(2)}, u32[]{:S(2)}) %collective-permute-start.2) | collective-permute-done | bytes 4128 | tf_op jit(solution)/shard_map/ppermute | solution.py:551
  56.5 20.5 %all_to_all.10.refs_0_ = f32[128,8,128]{2,1,0:T(8,128)S(1)} all-to-all(f32[128,8,128]{2,1,0:T(8,128)S(1)} %broadcast_in_dim.2), channel_id=1, replica_groups=mesh['file'=4,'rows'=32] {'file','rows'}, dimensions={0} | all-to-all | bytes 1048576 | tf_op jit(solution)/shard_map/all_to_all | solution.py:528
  77.1 6.0 %mix.1 = (f32[128,2048]{1,0:T(8,128)}, f32[128,2048]{1,0:T(8,128)}, f32[32,32]{1,0:T(8,128)}) custom-call(f32[128,8,128]{2,1,0:T(8,128)S(1)} %all_to_all.10.refs_0_, f32[2048,128]{1,0:T(8,128)S(1)} %bitcast.15, f32[2048,128]{1,0:T(8,128)S(1)} %bitcast.17), custom_call_target="tpu_custom_call" | custom-call | flops 33554432 | bytes 4194304 | tf_op jit(solution)/shard_map/mix/pallas_call | solution.py:514
  (2 shorter events, 0.0 us)
Async XLA Ops:
  0.6 39.6 %copy-start = (s32[128,8]{0,1:T(8,128)S(1)}, s32[128,8]{0,1:T(8,128)}, u32[]{:S(2)}) copy-start(s32[128,8]{0,1:T(8,128)} %param.7) | copy-start | bytes 12292
  4.4 30.4 %copy-start.2 = (s32[2,128]{1,0:T(2,128)S(1)}, s32[2,128]{1,0:T(2,128)}, u32[]{:S(2)}) copy-start(s32[2,128]{1,0:T(2,128)} %get-tuple-element.22.flags_ref.rows_ref) | copy-start | bytes 3076
  4.4 30.4 %all-to-all-start = ((f32[128,16,128]{2,1,0:T(8,128)}), f32[128,16,128]{2,1,0:T(8,128)S(1)}, u32[]{:S(2)}, u32[]{:S(2)}) async-start(f32[128,16,128]{2,1,0:T(8,128)} %get-tuple-element.21), calls=%async_computation | async-start | bytes 2097152 | tf_op jit(solution)/shard_map/all_to_all | solution.py:528
  15.9 0.7 copy-start.1
  35.8 4.4 %collective-permute-start = (f32[32,16,128]{2,1,0:T(8,128)S(1)}, f32[32,16,128]{2,1,0:T(8,128)S(1)}, u32[]{:S(2)}, u32[]{:S(2)}) collective-permute-start(f32[32,16,128]{2,1,0:T(8,128)S(1)} %get-tuple-element.27), channel_id=1, source_target_pairs={{0,1},{1,0},{2,3},{3,2},{4,5},{5,4},{6,7},{7,6},{8,9},{9,8},{10,11... | collective-permute-start | bytes 786440 | tf_op jit(solution)/shard_map/ppermute | solution.py:546
  37.1 12.7 %collective-permute-start.1 = (f32[32,16,128]{2,1,0:T(8,128)S(1)}, f32[32,16,128]{2,1,0:T(8,128)S(1)}, u32[]{:S(2)}, u32[]{:S(2)}) collective-permute-start(f32[32,16,128]{2,1,0:T(8,128)S(1)} %get-tuple-element.32), channel_id=1, source_target_pairs={{1,2},{2,1},{3,4},{4,3},{5,6},{6,5},{7,8},{8,7},{9,10},{10,9},{11,... | collective-permute-start | bytes 786440 | tf_op jit(solution)/shard_map/ppermute | solution.py:545
  55.3 1.2 %collective-permute-start.2 = (f32[8,128]{1,0:T(8,128)S(1)}, f32[8,128]{1,0:T(8,128)S(1)}, u32[]{:S(2)}, u32[]{:S(2)}) collective-permute-start(f32[8,128]{1,0:T(8,128)S(1)} %get-tuple-element.37), channel_id=1, source_target_pairs={{0,1},{1,0},{2,3},{3,2},{4,5},{5,4},{6,7},{7,6},{8,9},{9,8},{10,11... | collective-permute-start | bytes 12296 | tf_op jit(solution)/shard_map/ppermute | solution.py:551

commit v4 on v3

--- a/solution.py
+++ b/solution.py
@@ -218,27 +218,6 @@
         pairs_ref[HALF:NSNAP, sp * LANES : sp * LANES + LANES] = one
 
 
-def gram_kernel(snap_ref, tile_ref, pairs_ref):
-    make_pairs(snap_ref, pairs_ref)
-    pairs = pairs_ref[...]
-    gram = lax.dot_general(pairs, pairs, NT, precision=HIGH, preferred_element_type=jnp.float32)
-    tile_ref[...] = to_tile(gram)
-
-
-def gram_part(snaps):
-    slots = snaps.shape[0]
-    return pl.pallas_call(
-        gram_kernel,
-        out_shape=jax.ShapeDtypeStruct((8, LANES), jnp.float32),
-        in_specs=[spec(VMEM)],
-        out_specs=spec(VMEM),
-        scratch_shapes=[pltpu.VMEM((NSNAP, slots * BS), jnp.float32)],
-        compiler_params=limit(8),
-        cost_estimate=cost(2 * 6 * NSNAP * NSNAP * slots * BS, 3 * 1024 * 1024),
-        name="gram_part",
-    )(snaps)
-
-
 def fill(ref, xh_ref, xl_ref, base):
     low = low_half((HALF, LANES))
 
@@ -273,7 +252,7 @@
         fetch(at).start()
         return carry
 
-    lax.fori_loop(first * BATCH, last * BATCH, start, 0)
+    lax.fori_loop(first * BATCH, jnp.minimum(first + 1, last) * BATCH, start, 0)
     prepare()
 
     def table_row(n, s):
@@ -316,6 +295,7 @@
     red_ref[...] = jnp.zeros_like(red_ref)
 
     def batch(b, carry):
+        lax.fori_loop((b + 1) * BATCH, jnp.minimum(b + 2, last) * BATCH, start, 0)
         for j in range(BATCH):
             fetch(b * BATCH + j).wait()
         pairs, results = [], []
@@ -353,62 +333,81 @@
     run_batches(0, batches, cols_ref, own_ref, jac_hbm, out_ref, red_ref, xh_ref, xl_ref, jac_ref, order_ref, sems, prepare)
 
 
-def far_kernel(order_ref, cols_ref, near_ref, far_ref, own_ref, gram_ref, done_ref, red_in_ref, jac_hbm, out_ref, keep_ref, give_ref, red_ref, xh_ref, xl_ref, jac_ref, sems):
+def far_kernel(order_ref, cols_ref, far_ref, own_ref, done_ref, red_in_ref, th_ref, tl_ref, jac_hbm, out_ref, keep_ref, give_ref, red_ref, gram_ref, pairs_ref, table_sems, xh_ref, xl_ref, jac_ref, sems):
     slots = own_ref.shape[0]
     odd = my_part() % 2
 
     def prepare():
-        out_ref[...] = done_ref[...]
-        fill(near_ref, xh_ref, xl_ref, (1 - odd) * (slots + RIM))
-        fill(own_ref, xh_ref, xl_ref, RIM)
+        copies = (
+            pltpu.make_async_copy(th_ref, xh_ref, table_sems.at[0]),
+            pltpu.make_async_copy(tl_ref, xl_ref, table_sems.at[1]),
+            pltpu.make_async_copy(done_ref, out_ref, table_sems.at[2]),
+        )
+        for copy in copies:
+            copy.start()
+        make_pairs(own_ref, pairs_ref)
+        pairs = pairs_ref[...]
+        gram_ref[...] = lax.dot_general(pairs, pairs, NT, precision=HIGH, preferred_element_type=jnp.float32)
+        for copy in copies:
+            copy.wait()
         fill(far_ref, xh_ref, xl_ref, odd * (slots + RIM))
-        fill_zero(xh_ref, xl_ref)
 
     batches = order_ref[slots // GROUP]
     last = slots // GROUP // BATCH
     run_batches(batches, last, cols_ref, own_ref, jac_hbm, out_ref, red_ref, xh_ref, xl_ref, jac_ref, order_ref, sems, prepare)
 
-    gram = gram_ref[...]
+    gram = to_tile(gram_ref[...])
     reduced = to_tile(red_in_ref[...] + red_ref[...])
     keep_ref[...] = jnp.where(odd == 1, reduced, gram)
     give_ref[...] = jnp.where(odd == 1, gram, reduced)
 
 
-def scratch(slots, jac_split):
-    table = pltpu.VMEM((slots + 2 * RIM + 1, NSNAP, LANES), jnp.bfloat16)
-    return [table, table, pltpu.VMEM(jac_split.shape, jac_split.dtype), pltpu.SemaphoreType.DMA((slots // GROUP,))]
-
-
 def apply_near(order, cols, near, own, jac_split):
     slots = own.shape[0]
+    table = jax.ShapeDtypeStruct((slots + 2 * RIM + 1, NSNAP, LANES), jnp.bfloat16)
     return pl.pallas_call(
         near_kernel,
         out_shape=(
             jax.ShapeDtypeStruct((slots, HALF, LANES), jnp.float32),
             jax.ShapeDtypeStruct((NSNAP, NSNAP), jnp.float32),
+            table,
+            table,
         ),
         in_specs=[spec(SMEM)] * 2 + [spec(VMEM)] * 2 + [spec(pl.ANY)],
-        out_specs=(spec(VMEM),) * 2,
-        scratch_shapes=scratch(slots, jac_split),
-        compiler_params=limit(50),
+        out_specs=(spec(VMEM),) * 4,
+        scratch_shapes=[
+            pltpu.VMEM(jac_split.shape, jac_split.dtype),
+            pltpu.SemaphoreType.DMA((slots // GROUP,)),
+        ],
+        compiler_params=limit(46),
         cost_estimate=cost(2 * 3 * slots * 3 * NSNAP * 512 * BS, 20 * 1024 * 1024),
         name="apply_near",
     )(order, cols, near, own, jac_split)
 
 
-def apply_far(order, cols, near, far, own, gram, done, jac_split):
+def apply_far(order, cols, far, own, done, jac_split):
     slots = own.shape[0]
     tile = jax.ShapeDtypeStruct((8, LANES), jnp.float32)
+    table = pltpu.VMEM(done[2].shape, done[2].dtype)
     return pl.pallas_call(
         far_kernel,
         out_shape=(jax.ShapeDtypeStruct((slots, HALF, LANES), jnp.float32), tile, tile),
         in_specs=[spec(SMEM)] * 2 + [spec(VMEM)] * 6 + [spec(pl.ANY)],
         out_specs=(spec(VMEM),) * 3,
-        scratch_shapes=[pltpu.VMEM((NSNAP, NSNAP), jnp.float32)] + scratch(slots, jac_split),
-        compiler_params=limit(50),
+        scratch_shapes=[
+            pltpu.VMEM((NSNAP, NSNAP), jnp.float32),
+            pltpu.VMEM((NSNAP, NSNAP), jnp.float32),
+            pltpu.VMEM((NSNAP, slots * BS), jnp.float32),
+            pltpu.SemaphoreType.DMA((3,)),
+            table,
+            table,
+            pltpu.VMEM(jac_split.shape, jac_split.dtype),
+            pltpu.SemaphoreType.DMA((slots // GROUP,)),
+        ],
+        compiler_params=limit(46),
         cost_estimate=cost(2 * 3 * slots * NSNAP * 512 * BS, 8 * 1024 * 1024),
         name="apply_far",
-    )(order, cols, near, far, own, gram, *done, jac_split)
+    )(order, cols, far, own, *done, jac_split)
 
 
 def factor(gram, total_rows):
@@ -421,7 +420,7 @@
         for v in groups
     ]
     row_of = lambda x, p: jnp.broadcast_to(x[p // 8][p % 8 : p % 8 + 1, :], (8, LANES))
-    step = 4
+    step = 8
     for first in range(0, NSNAP, step):
         at = [(k % 2) * HALF + k // 2 for k in range(first, first + step)]
         rows = [row_of(work, p) for p in at]
@@ -544,10 +543,9 @@
     far_swap = [(p, ((p + 1) ^ 1) - 1) for p in range(1, n_part - 1)]
     far = lax.ppermute(far, AXES, far_swap)
     near = lax.ppermute(near, AXES, near_swap)
-    gram = gram_part(snaps)
     done = apply_near(order, cols, near, snaps, jac_split)
     done, far = lax.optimization_barrier((done, far))
-    jac_snaps, keep, give = apply_far(order, cols, near, far, snaps, gram, done, jac_split)
+    jac_snaps, keep, give = apply_far(order, cols, far, snaps, done, jac_split)
     pair_sum = keep + lax.ppermute(give, AXES, near_swap)
     sums = exchange(jnp.broadcast_to(pair_sum[None], (n_part, 8, LANES)))
     return mix(sums, snaps, jac_snaps, total_rows)

time: 83.4 us -> 81.9 us (0.982)
  Pallas kernels: 41.8 us -> 40.3 us
    pallas_call x1 -> x0, Pallas kernels: 1.12 us -> none  [gram_part(): pl.pallas_call(gram_kernel, out_shape=jax.ShapeDtypeStruct((8, LANES), jn...]
  transfers between devices with their start and end apart: 4 -> 4, of which waited for: 2 -> 2; matrix products, arithmetic and copies ran while one was open for 0% -> 0% of each run, Pallas kernels for 31% -> 30%
where the time goes in v4:
time: 81.9 us; the launch traced here: 81.5 us
  Pallas kernels  40.3 us (49%)
  blocking collectives  20.5 us (25%)
  starting transfers between devices  14.9 us (18%)
  waiting for transfers between devices  4.4 us (5%)
    all_to_all x1, blocking collectives, exchange(): return lax.all_to_all(tiles, AXES, split_axis=0, concat_axis=0, tiled=True)  20.5 us
    pallas_call x1, Pallas kernels, split_blocks(): pl.pallas_call(split_kernel, out_shape=(out, jax.ShapeDtypeStruct((slots...  15 us
    all_to_all x1, starting transfers between devices, exchange(): return lax.all_to_all(tiles, AXES, split_axis=0, concat_axis=0, tiled=True)  11.5 us
    pallas_call x1, Pallas kernels, apply_near(): pl.pallas_call(near_kernel, out_shape=(jax.ShapeDtypeStruct((slots, HALF,...  9.58 us
    pallas_call x1, Pallas kernels, mix(): pl.pallas_call(lambda *refs: mix_kernel(total_rows, *refs), out_shape=(ou...  5.68 us
    pallas_call x1, Pallas kernels, apply_far(): pl.pallas_call(far_kernel, out_shape=(jax.ShapeDtypeStruct((slots, HALF,...  5.35 us
    pallas_call x1, Pallas kernels, pack(): pl.pallas_call(pack_kernel, out_shape=(jax.ShapeDtypeStruct((n_part, per_...  3.76 us
    all_to_all x1, waiting for transfers between devices, exchange(): return lax.all_to_all(tiles, AXES, split_axis=0, concat_axis=0, tiled=True)  3.24 us
  transfers between devices with their start and end apart: 4, of which 2 were waited for; matrix products, arithmetic and copies ran while one was open for 0% of the time, Pallas kernels for 30%

profile of v4, /device:TPU:1, one launch (start us, length us, event | category | flops | bytes accessed | tf_op | source)
XLA Modules:
  0.0 81.5 jit_solution(11857017444572618461)
XLA Ops:
  0.6 0.0 copy-start
  0.6 3.8 %pack.1 = (f32[128,16,128]{2,1,0:T(8,128)}, s32[2,128]{1,0:T(2,128)}) custom-call(s32[128,128]{1,0:T(8,128)} %bitcast.23, s32[8,128]{1,0:T(8,128)} %bitcast.18, f32[2048,128]{1,0:T(8,128)} %bitcast.22), custom_call_target="tpu_custom_call" | custom-call | tf_op jit(solution)/shard_map/pack/pallas_call | solution.py:112
  4.4 0.0 copy-start.2
  4.4 11.5 %all-to-all-start = ((f32[128,16,128]{2,1,0:T(8,128)}), f32[128,16,128]{2,1,0:T(8,128)S(1)}, u32[]{:S(2)}, u32[]{:S(2)}) async-start(f32[128,16,128]{2,1,0:T(8,128)} %get-tuple-element.25), calls=%async_computation | async-start | bytes 2097152 | tf_op jit(solution)/shard_map/all_to_all | solution.py:527
  15.9 0.0 copy-start.1
  15.9 0.7 copy-done.1
  16.6 15.0 %split_blocks.1 = (bf16[128,2,64,512]{3,2,1,0:T(8,128)(2,1)}, s32[33]{0:T(128)S(1)}) custom-call(s32[2,128]{1,0:T(2,128)S(1)} %copy-done.1, f32[128,256,128]{2,1,0:T(8,128)} %bitcast.21), custom_call_target="tpu_custom_call" | custom-call | bytes 33554432 | tf_op jit(solution)/shard_map/split_blocks/pallas_call | solution.py:174
  31.6 3.2 %all-to-all-done = f32[128,16,128]{2,1,0:T(8,128)S(1)} async-done(((f32[128,16,128]{2,1,0:T(8,128)}), f32[128,16,128]{2,1,0:T(8,128)S(1)}, u32[]{:S(2)}, u32[]{:S(2)}) %all-to-all-start) | async-done | bytes 1048608 | tf_op jit(solution)/shard_map/all_to_all | solution.py:527
  34.8 0.0 copy-done.2
  34.8 0.9 %assemble.1 = (f32[128,16,128]{2,1,0:T(8,128)S(1)}, f32[32,16,128]{2,1,0:T(8,128)S(1)}, f32[32,16,128]{2,1,0:T(8,128)S(1)}) custom-call(s32[2,128]{1,0:T(2,128)S(1)} %copy-done.2, f32[2048,128]{1,0:T(8,128)S(1)} %bitcast.16), custom_call_target="tpu_custom_call" | custom-call | tf_op jit(solution)/shard_map/assemble/pallas_call | solution.py:204
  35.8 1.3 %collective-permute-start = (f32[32,16,128]{2,1,0:T(8,128)S(1)}, f32[32,16,128]{2,1,0:T(8,128)S(1)}, u32[]{:S(2)}, u32[]{:S(2)}) collective-permute-start(f32[32,16,128]{2,1,0:T(8,128)S(1)} %get-tuple-element.31), channel_id=1, source_target_pairs={{0,1},{1,0},{2,3},{3,2},{4,5},{5,4},{6,7},{7,6},{8,9},{9,8},{10,11... | collective-permute-start | bytes 786440 | tf_op jit(solution)/shard_map/ppermute | solution.py:545
  37.1 1.9 %collective-permute-start.1 = (f32[32,16,128]{2,1,0:T(8,128)S(1)}, f32[32,16,128]{2,1,0:T(8,128)S(1)}, u32[]{:S(2)}, u32[]{:S(2)}) collective-permute-start(f32[32,16,128]{2,1,0:T(8,128)S(1)} %get-tuple-element.38), channel_id=1, source_target_pairs={{1,2},{2,1},{3,4},{4,3},{5,6},{6,5},{7,8},{8,7},{9,10},{10,9},{11,... | collective-permute-start | bytes 786440 | tf_op jit(solution)/shard_map/ppermute | solution.py:544
  39.1 0.0 collective-permute-done.near_ref
  39.1 0.0 copy-done
  39.1 9.6 %apply_near.1 = (f32[128,16,128]{2,1,0:T(8,128)S(1)}, f32[32,32]{1,0:T(8,128)S(1)}, bf16[193,32,128]{2,1,0:T(8,128)(2,1)S(1)}, bf16[193,32,128]{2,1,0:T(8,128)(2,1)S(1)}) custom-call(s32[33]{0:T(128)S(1)} %get-tuple-element.29.order_ref, s32[8,128]{1,0:T(8,128)S(1)} %bitcast.19, f32[32,16,128]{2,1,0:T(8,128)S(1)} %collective-permute-done.near_ref, ...), custom_call_target="tpu_custom_call" | custom-call | flops 2415919104 | bytes 20971520 | tf_op jit(solution)/shard_map/apply_near/pallas_call | solution.py:368
  48.7 0.0 collective-permute-done.1.far_ref
  48.7 5.3 %apply_far.1 = (f32[128,16,128]{2,1,0:T(8,128)S(1)}, f32[8,128]{1,0:T(8,128)S(1)}, f32[8,128]{1,0:T(8,128)S(1)}) custom-call(s32[33]{0:T(128)S(1)} %get-tuple-element.29.order_ref, s32[8,128]{1,0:T(8,128)S(1)} %bitcast.20, f32[32,16,128]{2,1,0:T(8,128)S(1)} %collective-permute-done.1.far_ref, f32[128,16,128]{2,1,0:T(8,128)S(1)} %get-tuple-element.32.own_ref, ...), custom_call_target="tpu_custom_call" | custom-call | flops 805306368 | bytes 8388608 | tf_op jit(solution)/shard_map/apply_far/pallas_call | solution.py:392
  54.0 0.1 collective-permute-start.2
  54.1 1.2 %collective-permute-done.2 = f32[8,128]{1,0:T(8,128)S(1)} collective-permute-done((f32[8,128]{1,0:T(8,128)S(1)}, f32[8,128]{1,0:T(8,128)S(1)}, u32[]{:S(2)}, u32[]{:S(2)}) %collective-permute-start.2) | collective-permute-done | bytes 4128 | tf_op jit(solution)/shard_map/ppermute | solution.py:549
  55.3 20.5 %all_to_all.10.refs_0_ = f32[128,8,128]{2,1,0:T(8,128)S(1)} all-to-all(f32[128,8,128]{2,1,0:T(8,128)S(1)} %broadcast_in_dim.2), channel_id=1, replica_groups=mesh['file'=4,'rows'=32] {'file','rows'}, dimensions={0} | all-to-all | bytes 1048576 | tf_op jit(solution)/shard_map/all_to_all | solution.py:527
  75.8 5.7 %mix.1 = (f32[128,2048]{1,0:T(8,128)}, f32[128,2048]{1,0:T(8,128)}, f32[32,32]{1,0:T(8,128)}) custom-call(f32[128,8,128]{2,1,0:T(8,128)S(1)} %all_to_all.10.refs_0_, f32[2048,128]{1,0:T(8,128)S(1)} %bitcast.15, f32[2048,128]{1,0:T(8,128)S(1)} %bitcast.17), custom_call_target="tpu_custom_call" | custom-call | flops 33554432 | bytes 4194304 | tf_op jit(solution)/shard_map/mix/pallas_call | solution.py:513
  (2 shorter events, 0.0 us)
Async XLA Ops:
  0.6 38.4 %copy-start = (s32[128,8]{0,1:T(8,128)S(1)}, s32[128,8]{0,1:T(8,128)}, u32[]{:S(2)}) copy-start(s32[128,8]{0,1:T(8,128)} %param.7) | copy-start | bytes 12292
  4.4 30.4 %copy-start.2 = (s32[2,128]{1,0:T(2,128)S(1)}, s32[2,128]{1,0:T(2,128)}, u32[]{:S(2)}) copy-start(s32[2,128]{1,0:T(2,128)} %get-tuple-element.26.flags_ref.rows_ref) | copy-start | bytes 3076
  4.4 30.4 %all-to-all-start = ((f32[128,16,128]{2,1,0:T(8,128)}), f32[128,16,128]{2,1,0:T(8,128)S(1)}, u32[]{:S(2)}, u32[]{:S(2)}) async-start(f32[128,16,128]{2,1,0:T(8,128)} %get-tuple-element.25), calls=%async_computation | async-start | bytes 2097152 | tf_op jit(solution)/shard_map/all_to_all | solution.py:527
  15.9 0.7 copy-start.1
  35.8 3.3 %collective-permute-start = (f32[32,16,128]{2,1,0:T(8,128)S(1)}, f32[32,16,128]{2,1,0:T(8,128)S(1)}, u32[]{:S(2)}, u32[]{:S(2)}) collective-permute-start(f32[32,16,128]{2,1,0:T(8,128)S(1)} %get-tuple-element.31), channel_id=1, source_target_pairs={{0,1},{1,0},{2,3},{3,2},{4,5},{5,4},{6,7},{7,6},{8,9},{9,8},{10,11... | collective-permute-start | bytes 786440 | tf_op jit(solution)/shard_map/ppermute | solution.py:545
  37.1 11.6 %collective-permute-start.1 = (f32[32,16,128]{2,1,0:T(8,128)S(1)}, f32[32,16,128]{2,1,0:T(8,128)S(1)}, u32[]{:S(2)}, u32[]{:S(2)}) collective-permute-start(f32[32,16,128]{2,1,0:T(8,128)S(1)} %get-tuple-element.38), channel_id=1, source_target_pairs={{1,2},{2,1},{3,4},{4,3},{5,6},{6,5},{7,8},{8,7},{9,10},{10,9},{11,... | collective-permute-start | bytes 786440 | tf_op jit(solution)/shard_map/ppermute | solution.py:544
  54.0 1.2 %collective-permute-start.2 = (f32[8,128]{1,0:T(8,128)S(1)}, f32[8,128]{1,0:T(8,128)S(1)}, u32[]{:S(2)}, u32[]{:S(2)}) collective-permute-start(f32[8,128]{1,0:T(8,128)S(1)} %get-tuple-element.45), channel_id=1, source_target_pairs={{0,1},{1,0},{2,3},{3,2},{4,5},{5,4},{6,7},{7,6},{8,9},{9,8},{10,11... | collective-permute-start | bytes 12296 | tf_op jit(solution)/shard_map/ppermute | solution.py:549

commit v5 on v4

--- a/solution.py
+++ b/solution.py
@@ -98,7 +98,7 @@
             out_ref[part, 4 * q : 4 * q + 4, :] = snap_ref[pl.ds(row, 4, stride=8), :]
         return carry
 
-    lax.fori_loop(0, n_part, body, 0, unroll=8)
+    lax.fori_loop(0, n_part, body, 0, unroll=16)
 
 
 def pack(snapshots, part_map, cols, n_part):
@@ -193,7 +193,7 @@
             snap_ref[s, 4 * f : 4 * f + 4, :] = recv_ref[pl.ds(f * per_file + row, 4), :]
         return carry
 
-    lax.fori_loop(0, slots, body, 0, unroll=8)
+    lax.fori_loop(0, slots, body, 0, unroll=16)
     odd = my_part() % 2
     near_ref[...] = snap_ref[pl.ds((1 - odd) * (slots - RIM), RIM)]
     far_ref[...] = snap_ref[pl.ds(odd * (slots - RIM), RIM)]
@@ -501,7 +501,7 @@
                         target[rows, LANES * k2 : LANES * k2 + LANES] = totals[k2, h]
             return carry
 
-        lax.fori_loop(0, target.shape[0] // 16, body, 0)
+        lax.fori_loop(0, target.shape[0] // 16, body, 0, unroll=2)
 
 
 def mix(sums, snaps, jac, total_rows):

time: 81.9 us -> 81.4 us (level)
  no operation moved by 1% of the time
where the time goes in v5:
time: 81.4 us; the launch traced here: 81.1 us
  Pallas kernels  39.8 us (49%)
  blocking collectives  20.5 us (25%)
  starting transfers between devices  14.9 us (18%)
  waiting for transfers between devices  4.4 us (5%)
    all_to_all x1, blocking collectives, exchange(): return lax.all_to_all(tiles, AXES, split_axis=0, concat_axis=0, tiled=True)  20.5 us
    pallas_call x1, Pallas kernels, split_blocks(): pl.pallas_call(split_kernel, out_shape=(out, jax.ShapeDtypeStruct((slots...  15 us
    all_to_all x1, starting transfers between devices, exchange(): return lax.all_to_all(tiles, AXES, split_axis=0, concat_axis=0, tiled=True)  11.5 us
    pallas_call x1, Pallas kernels, apply_near(): pl.pallas_call(near_kernel, out_shape=(jax.ShapeDtypeStruct((slots, HALF,...  9.58 us
    pallas_call x1, Pallas kernels, apply_far(): pl.pallas_call(far_kernel, out_shape=(jax.ShapeDtypeStruct((slots, HALF,...  5.35 us
    pallas_call x1, Pallas kernels, mix(): pl.pallas_call(lambda *refs: mix_kernel(total_rows, *refs), out_shape=(ou...  5.33 us
    pallas_call x1, Pallas kernels, pack(): pl.pallas_call(pack_kernel, out_shape=(jax.ShapeDtypeStruct((n_part, per_...  3.71 us
    all_to_all x1, waiting for transfers between devices, exchange(): return lax.all_to_all(tiles, AXES, split_axis=0, concat_axis=0, tiled=True)  3.24 us
  transfers between devices with their start and end apart: 4, of which 2 were waited for; matrix products, arithmetic and copies ran while one was open for 0% of the time, Pallas kernels for 30%

profile of v5, /device:TPU:1, one launch (start us, length us, event | category | flops | bytes accessed | tf_op | source)
XLA Modules:
  0.0 81.1 jit_solution(5058835487250528112)
XLA Ops:
  0.6 0.0 copy-start
  0.6 3.7 %pack.1 = (f32[128,16,128]{2,1,0:T(8,128)}, s32[2,128]{1,0:T(2,128)}) custom-call(s32[128,128]{1,0:T(8,128)} %bitcast.23, s32[8,128]{1,0:T(8,128)} %bitcast.18, f32[2048,128]{1,0:T(8,128)} %bitcast.22), custom_call_target="tpu_custom_call" | custom-call | tf_op jit(solution)/shard_map/pack/pallas_call | solution.py:112
  4.4 0.0 copy-start.2
  4.4 11.5 %all-to-all-start = ((f32[128,16,128]{2,1,0:T(8,128)}), f32[128,16,128]{2,1,0:T(8,128)S(1)}, u32[]{:S(2)}, u32[]{:S(2)}) async-start(f32[128,16,128]{2,1,0:T(8,128)} %get-tuple-element.25), calls=%async_computation | async-start | bytes 2097152 | tf_op jit(solution)/shard_map/all_to_all | solution.py:527
  15.9 0.0 copy-start.1
  15.9 0.7 copy-done.1
  16.6 15.0 %split_blocks.1 = (bf16[128,2,64,512]{3,2,1,0:T(8,128)(2,1)}, s32[33]{0:T(128)S(1)}) custom-call(s32[2,128]{1,0:T(2,128)S(1)} %copy-done.1, f32[128,256,128]{2,1,0:T(8,128)} %bitcast.21), custom_call_target="tpu_custom_call" | custom-call | bytes 33554432 | tf_op jit(solution)/shard_map/split_blocks/pallas_call | solution.py:174
  31.5 3.2 %all-to-all-done = f32[128,16,128]{2,1,0:T(8,128)S(1)} async-done(((f32[128,16,128]{2,1,0:T(8,128)}), f32[128,16,128]{2,1,0:T(8,128)S(1)}, u32[]{:S(2)}, u32[]{:S(2)}) %all-to-all-start) | async-done | bytes 1048608 | tf_op jit(solution)/shard_map/all_to_all | solution.py:527
  34.8 0.0 copy-done.2
  34.8 0.9 %assemble.1 = (f32[128,16,128]{2,1,0:T(8,128)S(1)}, f32[32,16,128]{2,1,0:T(8,128)S(1)}, f32[32,16,128]{2,1,0:T(8,128)S(1)}) custom-call(s32[2,128]{1,0:T(2,128)S(1)} %copy-done.2, f32[2048,128]{1,0:T(8,128)S(1)} %bitcast.16), custom_call_target="tpu_custom_call" | custom-call | tf_op jit(solution)/shard_map/assemble/pallas_call | solution.py:204
  35.7 1.3 %collective-permute-start = (f32[32,16,128]{2,1,0:T(8,128)S(1)}, f32[32,16,128]{2,1,0:T(8,128)S(1)}, u32[]{:S(2)}, u32[]{:S(2)}) collective-permute-start(f32[32,16,128]{2,1,0:T(8,128)S(1)} %get-tuple-element.31), channel_id=1, source_target_pairs={{0,1},{1,0},{2,3},{3,2},{4,5},{5,4},{6,7},{7,6},{8,9},{9,8},{10,11... | collective-permute-start | bytes 786440 | tf_op jit(solution)/shard_map/ppermute | solution.py:545
  37.0 1.9 %collective-permute-start.1 = (f32[32,16,128]{2,1,0:T(8,128)S(1)}, f32[32,16,128]{2,1,0:T(8,128)S(1)}, u32[]{:S(2)}, u32[]{:S(2)}) collective-permute-start(f32[32,16,128]{2,1,0:T(8,128)S(1)} %get-tuple-element.38), channel_id=1, source_target_pairs={{1,2},{2,1},{3,4},{4,3},{5,6},{6,5},{7,8},{8,7},{9,10},{10,9},{11,... | collective-permute-start | bytes 786440 | tf_op jit(solution)/shard_map/ppermute | solution.py:544
  39.0 0.0 collective-permute-done.near_ref
  39.0 0.0 copy-done
  39.0 9.6 %apply_near.1 = (f32[128,16,128]{2,1,0:T(8,128)S(1)}, f32[32,32]{1,0:T(8,128)S(1)}, bf16[193,32,128]{2,1,0:T(8,128)(2,1)S(1)}, bf16[193,32,128]{2,1,0:T(8,128)(2,1)S(1)}) custom-call(s32[33]{0:T(128)S(1)} %get-tuple-element.29.order_ref, s32[8,128]{1,0:T(8,128)S(1)} %bitcast.19, f32[32,16,128]{2,1,0:T(8,128)S(1)} %collective-permute-done.near_ref, ...), custom_call_target="tpu_custom_call" | custom-call | flops 2415919104 | bytes 20971520 | tf_op jit(solution)/shard_map/apply_near/pallas_call | solution.py:368
  48.6 0.0 collective-permute-done.1.far_ref
  48.6 5.3 %apply_far.1 = (f32[128,16,128]{2,1,0:T(8,128)S(1)}, f32[8,128]{1,0:T(8,128)S(1)}, f32[8,128]{1,0:T(8,128)S(1)}) custom-call(s32[33]{0:T(128)S(1)} %get-tuple-element.29.order_ref, s32[8,128]{1,0:T(8,128)S(1)} %bitcast.20, f32[32,16,128]{2,1,0:T(8,128)S(1)} %collective-permute-done.1.far_ref, f32[128,16,128]{2,1,0:T(8,128)S(1)} %get-tuple-element.32.own_ref, ...), custom_call_target="tpu_custom_call" | custom-call | flops 805306368 | bytes 8388608 | tf_op jit(solution)/shard_map/apply_far/pallas_call | solution.py:392
  54.0 0.1 collective-permute-start.2
  54.0 1.2 %collective-permute-done.2 = f32[8,128]{1,0:T(8,128)S(1)} collective-permute-done((f32[8,128]{1,0:T(8,128)S(1)}, f32[8,128]{1,0:T(8,128)S(1)}, u32[]{:S(2)}, u32[]{:S(2)}) %collective-permute-start.2) | collective-permute-done | bytes 4128 | tf_op jit(solution)/shard_map/ppermute | solution.py:549
  55.2 20.5 %all_to_all.10.refs_0_ = f32[128,8,128]{2,1,0:T(8,128)S(1)} all-to-all(f32[128,8,128]{2,1,0:T(8,128)S(1)} %broadcast_in_dim.2), channel_id=1, replica_groups=mesh['file'=4,'rows'=32] {'file','rows'}, dimensions={0} | all-to-all | bytes 1048576 | tf_op jit(solution)/shard_map/all_to_all | solution.py:527
  75.7 5.3 %mix.1 = (f32[128,2048]{1,0:T(8,128)}, f32[128,2048]{1,0:T(8,128)}, f32[32,32]{1,0:T(8,128)}) custom-call(f32[128,8,128]{2,1,0:T(8,128)S(1)} %all_to_all.10.refs_0_, f32[2048,128]{1,0:T(8,128)S(1)} %bitcast.15, f32[2048,128]{1,0:T(8,128)S(1)} %bitcast.17), custom_call_target="tpu_custom_call" | custom-call | flops 33554432 | bytes 4194304 | tf_op jit(solution)/shard_map/mix/pallas_call | solution.py:513
  (2 shorter events, 0.0 us)
Async XLA Ops:
  0.6 38.4 %copy-start = (s32[128,8]{0,1:T(8,128)S(1)}, s32[128,8]{0,1:T(8,128)}, u32[]{:S(2)}) copy-start(s32[128,8]{0,1:T(8,128)} %param.7) | copy-start | bytes 12292
  4.4 30.4 %copy-start.2 = (s32[2,128]{1,0:T(2,128)S(1)}, s32[2,128]{1,0:T(2,128)}, u32[]{:S(2)}) copy-start(s32[2,128]{1,0:T(2,128)} %get-tuple-element.26.flags_ref.rows_ref) | copy-start | bytes 3076
  4.4 30.4 %all-to-all-start = ((f32[128,16,128]{2,1,0:T(8,128)}), f32[128,16,128]{2,1,0:T(8,128)S(1)}, u32[]{:S(2)}, u32[]{:S(2)}) async-start(f32[128,16,128]{2,1,0:T(8,128)} %get-tuple-element.25), calls=%async_computation | async-start | bytes 2097152 | tf_op jit(solution)/shard_map/all_to_all | solution.py:527
  15.9 0.7 copy-start.1
  35.7 3.3 %collective-permute-start = (f32[32,16,128]{2,1,0:T(8,128)S(1)}, f32[32,16,128]{2,1,0:T(8,128)S(1)}, u32[]{:S(2)}, u32[]{:S(2)}) collective-permute-start(f32[32,16,128]{2,1,0:T(8,128)S(1)} %get-tuple-element.31), channel_id=1, source_target_pairs={{0,1},{1,0},{2,3},{3,2},{4,5},{5,4},{6,7},{7,6},{8,9},{9,8},{10,11... | collective-permute-start | bytes 786440 | tf_op jit(solution)/shard_map/ppermute | solution.py:545
  37.0 11.6 %collective-permute-start.1 = (f32[32,16,128]{2,1,0:T(8,128)S(1)}, f32[32,16,128]{2,1,0:T(8,128)S(1)}, u32[]{:S(2)}, u32[]{:S(2)}) collective-permute-start(f32[32,16,128]{2,1,0:T(8,128)S(1)} %get-tuple-element.38), channel_id=1, source_target_pairs={{1,2},{2,1},{3,4},{4,3},{5,6},{6,5},{7,8},{8,7},{9,10},{10,9},{11,... | collective-permute-start | bytes 786440 | tf_op jit(solution)/shard_map/ppermute | solution.py:544
  54.0 1.2 %collective-permute-start.2 = (f32[8,128]{1,0:T(8,128)S(1)}, f32[8,128]{1,0:T(8,128)S(1)}, u32[]{:S(2)}, u32[]{:S(2)}) collective-permute-start(f32[8,128]{1,0:T(8,128)S(1)} %get-tuple-element.45), channel_id=1, source_target_pairs={{0,1},{1,0},{2,3},{3,2},{4,5},{5,4},{6,7},{7,6},{8,9},{9,8},{10,11... | collective-permute-start | bytes 12296 | tf_op jit(solution)/shard_map/ppermute | solution.py:549

commit v6 on v5

--- a/solution.py
+++ b/solution.py
@@ -162,7 +162,7 @@
                     out_ref[s, 1, rows, lanes] = low
         return carry
 
-    lax.fori_loop(0, jac_ref.shape[0], body, 0, unroll=4)
+    lax.fori_loop(0, jac_ref.shape[0], body, 0, unroll=8)
 
 
 def split_blocks(jac_blocks, flags):

time: 81.4 us -> 81.4 us (level)
  transfers between devices with their start and end apart: 4 -> 4, of which waited for: 2 -> 2; matrix products, arithmetic and copies ran while one was open for 0% -> 0% of each run, Pallas kernels for 30% -> 29%
where the time goes in v6:
time: 81.4 us; the launch traced here: 81.1 us
  Pallas kernels  39 us (48%)
  blocking collectives  20.5 us (25%)
  starting transfers between devices  14.9 us (18%)
  waiting for transfers between devices  5.2 us (6%)
    all_to_all x1, blocking collectives, exchange(): return lax.all_to_all(tiles, AXES, split_axis=0, concat_axis=0, tiled=True)  20.5 us
    pallas_call x1, Pallas kernels, split_blocks(): pl.pallas_call(split_kernel, out_shape=(out, jax.ShapeDtypeStruct((slots...  14.2 us
    all_to_all x1, starting transfers between devices, exchange(): return lax.all_to_all(tiles, AXES, split_axis=0, concat_axis=0, tiled=True)  11.5 us
    pallas_call x1, Pallas kernels, apply_near(): pl.pallas_call(near_kernel, out_shape=(jax.ShapeDtypeStruct((slots, HALF,...  9.58 us
    pallas_call x1, Pallas kernels, apply_far(): pl.pallas_call(far_kernel, out_shape=(jax.ShapeDtypeStruct((slots, HALF,...  5.35 us
    pallas_call x1, Pallas kernels, mix(): pl.pallas_call(lambda *refs: mix_kernel(total_rows, *refs), out_shape=(ou...  5.33 us
    all_to_all x1, waiting for transfers between devices, exchange(): return lax.all_to_all(tiles, AXES, split_axis=0, concat_axis=0, tiled=True)  4.05 us
    pallas_call x1, Pallas kernels, pack(): pl.pallas_call(pack_kernel, out_shape=(jax.ShapeDtypeStruct((n_part, per_...  3.71 us
  transfers between devices with their start and end apart: 4, of which 2 were waited for; matrix products, arithmetic and copies ran while one was open for 0% of the time, Pallas kernels for 29%

profile of v6, /device:TPU:1, one launch (start us, length us, event | category | flops | bytes accessed | tf_op | source)
XLA Modules:
  0.0 81.1 jit_solution(13357579949084085934)
XLA Ops:
  0.6 0.0 copy-start
  0.6 3.7 %pack.1 = (f32[128,16,128]{2,1,0:T(8,128)}, s32[2,128]{1,0:T(2,128)}) custom-call(s32[128,128]{1,0:T(8,128)} %bitcast.23, s32[8,128]{1,0:T(8,128)} %bitcast.18, f32[2048,128]{1,0:T(8,128)} %bitcast.22), custom_call_target="tpu_custom_call" | custom-call | tf_op jit(solution)/shard_map/pack/pallas_call | solution.py:112
  4.4 0.0 copy-start.2
  4.4 11.5 %all-to-all-start = ((f32[128,16,128]{2,1,0:T(8,128)}), f32[128,16,128]{2,1,0:T(8,128)S(1)}, u32[]{:S(2)}, u32[]{:S(2)}) async-start(f32[128,16,128]{2,1,0:T(8,128)} %get-tuple-element.25), calls=%async_computation | async-start | bytes 2097152 | tf_op jit(solution)/shard_map/all_to_all | solution.py:527
  15.9 0.0 copy-start.1
  15.9 0.7 copy-done.1
  16.6 14.2 %split_blocks.1 = (bf16[128,2,64,512]{3,2,1,0:T(8,128)(2,1)}, s32[33]{0:T(128)S(1)}) custom-call(s32[2,128]{1,0:T(2,128)S(1)} %copy-done.1, f32[128,256,128]{2,1,0:T(8,128)} %bitcast.21), custom_call_target="tpu_custom_call" | custom-call | bytes 33554432 | tf_op jit(solution)/shard_map/split_blocks/pallas_call | solution.py:174
  30.7 4.0 %all-to-all-done = f32[128,16,128]{2,1,0:T(8,128)S(1)} async-done(((f32[128,16,128]{2,1,0:T(8,128)}), f32[128,16,128]{2,1,0:T(8,128)S(1)}, u32[]{:S(2)}, u32[]{:S(2)}) %all-to-all-start) | async-done | bytes 1048608 | tf_op jit(solution)/shard_map/all_to_all | solution.py:527
  34.8 0.0 copy-done.2
  34.8 0.9 %assemble.1 = (f32[128,16,128]{2,1,0:T(8,128)S(1)}, f32[32,16,128]{2,1,0:T(8,128)S(1)}, f32[32,16,128]{2,1,0:T(8,128)S(1)}) custom-call(s32[2,128]{1,0:T(2,128)S(1)} %copy-done.2, f32[2048,128]{1,0:T(8,128)S(1)} %bitcast.16), custom_call_target="tpu_custom_call" | custom-call | tf_op jit(solution)/shard_map/assemble/pallas_call | solution.py:204
  35.7 1.3 %collective-permute-start = (f32[32,16,128]{2,1,0:T(8,128)S(1)}, f32[32,16,128]{2,1,0:T(8,128)S(1)}, u32[]{:S(2)}, u32[]{:S(2)}) collective-permute-start(f32[32,16,128]{2,1,0:T(8,128)S(1)} %get-tuple-element.31), channel_id=1, source_target_pairs={{0,1},{1,0},{2,3},{3,2},{4,5},{5,4},{6,7},{7,6},{8,9},{9,8},{10,11... | collective-permute-start | bytes 786440 | tf_op jit(solution)/shard_map/ppermute | solution.py:545
  37.0 1.9 %collective-permute-start.1 = (f32[32,16,128]{2,1,0:T(8,128)S(1)}, f32[32,16,128]{2,1,0:T(8,128)S(1)}, u32[]{:S(2)}, u32[]{:S(2)}) collective-permute-start(f32[32,16,128]{2,1,0:T(8,128)S(1)} %get-tuple-element.38), channel_id=1, source_target_pairs={{1,2},{2,1},{3,4},{4,3},{5,6},{6,5},{7,8},{8,7},{9,10},{10,9},{11,... | collective-permute-start | bytes 786440 | tf_op jit(solution)/shard_map/ppermute | solution.py:544
  39.0 0.0 collective-permute-done.near_ref
  39.0 0.0 copy-done
  39.0 9.6 %apply_near.1 = (f32[128,16,128]{2,1,0:T(8,128)S(1)}, f32[32,32]{1,0:T(8,128)S(1)}, bf16[193,32,128]{2,1,0:T(8,128)(2,1)S(1)}, bf16[193,32,128]{2,1,0:T(8,128)(2,1)S(1)}) custom-call(s32[33]{0:T(128)S(1)} %get-tuple-element.29.order_ref, s32[8,128]{1,0:T(8,128)S(1)} %bitcast.19, f32[32,16,128]{2,1,0:T(8,128)S(1)} %collective-permute-done.near_ref, ...), custom_call_target="tpu_custom_call" | custom-call | flops 2415919104 | bytes 20971520 | tf_op jit(solution)/shard_map/apply_near/pallas_call | solution.py:368
  48.6 0.0 collective-permute-done.1.far_ref
  48.6 5.3 %apply_far.1 = (f32[128,16,128]{2,1,0:T(8,128)S(1)}, f32[8,128]{1,0:T(8,128)S(1)}, f32[8,128]{1,0:T(8,128)S(1)}) custom-call(s32[33]{0:T(128)S(1)} %get-tuple-element.29.order_ref, s32[8,128]{1,0:T(8,128)S(1)} %bitcast.20, f32[32,16,128]{2,1,0:T(8,128)S(1)} %collective-permute-done.1.far_ref, f32[128,16,128]{2,1,0:T(8,128)S(1)} %get-tuple-element.32.own_ref, ...), custom_call_target="tpu_custom_call" | custom-call | flops 805306368 | bytes 8388608 | tf_op jit(solution)/shard_map/apply_far/pallas_call | solution.py:392
  54.0 0.1 collective-permute-start.2
  54.0 1.2 %collective-permute-done.2 = f32[8,128]{1,0:T(8,128)S(1)} collective-permute-done((f32[8,128]{1,0:T(8,128)S(1)}, f32[8,128]{1,0:T(8,128)S(1)}, u32[]{:S(2)}, u32[]{:S(2)}) %collective-permute-start.2) | collective-permute-done | bytes 4128 | tf_op jit(solution)/shard_map/ppermute | solution.py:549
  55.2 20.5 %all_to_all.10.refs_0_ = f32[128,8,128]{2,1,0:T(8,128)S(1)} all-to-all(f32[128,8,128]{2,1,0:T(8,128)S(1)} %broadcast_in_dim.2), channel_id=1, replica_groups=mesh['file'=4,'rows'=32] {'file','rows'}, dimensions={0} | all-to-all | bytes 1048576 | tf_op jit(solution)/shard_map/all_to_all | solution.py:527
  75.7 5.3 %mix.1 = (f32[128,2048]{1,0:T(8,128)}, f32[128,2048]{1,0:T(8,128)}, f32[32,32]{1,0:T(8,128)}) custom-call(f32[128,8,128]{2,1,0:T(8,128)S(1)} %all_to_all.10.refs_0_, f32[2048,128]{1,0:T(8,128)S(1)} %bitcast.15, f32[2048,128]{1,0:T(8,128)S(1)} %bitcast.17), custom_call_target="tpu_custom_call" | custom-call | flops 33554432 | bytes 4194304 | tf_op jit(solution)/shard_map/mix/pallas_call | solution.py:513
  (2 shorter events, 0.0 us)
Async XLA Ops:
  0.6 38.4 %copy-start = (s32[128,8]{0,1:T(8,128)S(1)}, s32[128,8]{0,1:T(8,128)}, u32[]{:S(2)}) copy-start(s32[128,8]{0,1:T(8,128)} %param.7) | copy-start | bytes 12292
  4.4 30.4 %copy-start.2 = (s32[2,128]{1,0:T(2,128)S(1)}, s32[2,128]{1,0:T(2,128)}, u32[]{:S(2)}) copy-start(s32[2,128]{1,0:T(2,128)} %get-tuple-element.26.flags_ref.rows_ref) | copy-start | bytes 3076
  4.4 30.4 %all-to-all-start = ((f32[128,16,128]{2,1,0:T(8,128)}), f32[128,16,128]{2,1,0:T(8,128)S(1)}, u32[]{:S(2)}, u32[]{:S(2)}) async-start(f32[128,16,128]{2,1,0:T(8,128)} %get-tuple-element.25), calls=%async_computation | async-start | bytes 2097152 | tf_op jit(solution)/shard_map/all_to_all | solution.py:527
  15.9 0.7 copy-start.1
  35.7 3.3 %collective-permute-start = (f32[32,16,128]{2,1,0:T(8,128)S(1)}, f32[32,16,128]{2,1,0:T(8,128)S(1)}, u32[]{:S(2)}, u32[]{:S(2)}) collective-permute-start(f32[32,16,128]{2,1,0:T(8,128)S(1)} %get-tuple-element.31), channel_id=1, source_target_pairs={{0,1},{1,0},{2,3},{3,2},{4,5},{5,4},{6,7},{7,6},{8,9},{9,8},{10,11... | collective-permute-start | bytes 786440 | tf_op jit(solution)/shard_map/ppermute | solution.py:545
  37.0 11.6 %collective-permute-start.1 = (f32[32,16,128]{2,1,0:T(8,128)S(1)}, f32[32,16,128]{2,1,0:T(8,128)S(1)}, u32[]{:S(2)}, u32[]{:S(2)}) collective-permute-start(f32[32,16,128]{2,1,0:T(8,128)S(1)} %get-tuple-element.38), channel_id=1, source_target_pairs={{1,2},{2,1},{3,4},{4,3},{5,6},{6,5},{7,8},{8,7},{9,10},{10,9},{11,... | collective-permute-start | bytes 786440 | tf_op jit(solution)/shard_map/ppermute | solution.py:544
  54.0 1.2 %collective-permute-start.2 = (f32[8,128]{1,0:T(8,128)S(1)}, f32[8,128]{1,0:T(8,128)S(1)}, u32[]{:S(2)}, u32[]{:S(2)}) collective-permute-start(f32[8,128]{1,0:T(8,128)S(1)} %get-tuple-element.45), channel_id=1, source_target_pairs={{0,1},{1,0},{2,3},{3,2},{4,5},{5,4},{6,7},{7,6},{8,9},{9,8},{10,11... | collective-permute-start | bytes 12296 | tf_op jit(solution)/shard_map/ppermute | solution.py:549
